TPU v7x, 32 devices: a whole 2x2x4 slice. The times are simulated.
32 devices in a mesh: inline: 2 (over core), tile: 16 (over z, y, x).
Axes of the slice: x: 2, y: 2, z: 4, core: 2. Of those that a mesh axis runs over, the one named last changes fastest.
Arguments:
- features: bfloat16 [96, 4, 32, 128], P(None, 'inline', 'tile'), may hold values from -13 to 13
- conv1_weight: bfloat16 [96, 27, 96], replicated, may hold values from -0.125 to 0.125
- conv2_weight: bfloat16 [96, 27, 96], replicated, may hold values from -0.125 to 0.125
- fault_head: bfloat16 [96, 2], replicated, may hold values from -0.625 to 0.625
- horizon_head: bfloat16 [96, 4], replicated, may hold values from -0.625 to 0.625
- salt_query: bfloat16 [96], replicated, may hold values from -0.625 to 0.625
- salt_head: bfloat16 [96, 2], replicated, may hold values from -0.625 to 0.625
- fault_labels: int32 [4, 32, 128], P('inline', 'tile'), may hold values from 0 to 1
- horizon_labels: int32 [4, 32, 128], P('inline', 'tile'), may hold values from 0 to 3
- salt_labels: int32 [4, 128], P('inline'), may hold values from 0 to 1
Outputs:
- grads: float32 [2, 3, 248832], P(None, None, ('inline', 'tile'))
- gram: float32 [2, 3, 3], replicated
All inputs are finite; a program needn't handle non-finite values.
Results may differ from a plain program's by a relative error of at most 0.0043.
Values may be sent and summed in bfloat16 or wider, within the bound.
No kernel may reach another device: no remote copies, remote signals or barrier semaphores. Data moves between devices by JAX's collectives and lax.ppermute only.
A program may use at most 128 MiB of HBM per device.

v0:
```python
import functools
import math

import jax
import jax.numpy as jnp
from jax import lax
from jax.experimental import pallas as pl
from jax.experimental.pallas import tpu as pltpu
from jax.experimental.layout import Layout, with_layout_constraint
from jax.sharding import PartitionSpec as P


D1 = 1
D2 = 2
REACH = D1 + 2 * D2

CAPPING = 8.0
LABEL_ROWS = 8
AXES = ("inline", "tile")


def round_up(value, unit):
    return -(-value // unit) * unit


def bits(count):
    return [1 << bit for bit in range(count.bit_length() - 1)]


def swap_pairs(count, distance):
    return [(i, i ^ distance) for i in range(count)]


def window(cells, axis, dim, halo):
    count, length = (lax.axis_size(axis), cells.shape[dim])
    covered, hops = (0, 1)
    while covered < halo:
        amount = min(halo - covered, length + covered)
        size = cells.shape[dim]
        start = lax.slice_in_dim(cells, covered, covered + amount, axis=dim)
        end = lax.slice_in_dim(cells, size - covered - amount, size - covered, axis=dim)
        up = [(i, i + hops) for i in range(count - hops)]
        down = [(j, i) for i, j in up]
        before = lax.ppermute(end, axis, up)
        after = lax.ppermute(start, axis, down)
        cells = jnp.concatenate([before, cells, after], axis=dim)
        covered += amount
        hops = covered // length + 1
    return cells


def outward(cells, halo, needed, riders):
    ready = []
    here, length = (lax.axis_index("inline"), cells.shape[1])
    count = lax.axis_size("tile")
    chain = jnp.where(here == 0, cells[:, ::-1], cells)
    side = None
    covered, hops = (0, 1)
    while covered < halo:
        amount = min(halo - covered, length + covered)
        pairs = [(i, i + hops) for i in range(count - hops)]
        pairs += [(count + j, count + i) for i, j in pairs]
        taken = lax.ppermute(chain[:, :amount], AXES, pairs)
        if riders:
            taken, *made = lax.optimization_barrier((taken, *riders.pop(0)))
            ready += made
        side = taken if side is None else jnp.concatenate([side, taken], axis=1)
        chain = jnp.concatenate([chain, taken], axis=1)
        covered += amount
        hops = covered // length + 1
    for group in riders:
        ready += group
    other = lax.ppermute(side[:, :needed], "inline", [(0, 1), (1, 0)])
    return side, other, ready


def share_sums(value, axes):
    copies = jnp.broadcast_to(value, (lax.axis_size(axes),) + value.shape)
    return jnp.sum(lax.all_to_all(copies, axes, 0, 0), axis=0)


def halving_order(first):
    tile = bits(lax.axis_size("tile"))
    tile = tile[first : first + 1] + tile[:first] + tile[first + 1 :]
    inline = [("inline", distance) for distance in bits(lax.axis_size("inline"))]
    return inline + [("tile", distance) for distance in tile]


def halve(kept, axis, distance):
    half = kept.shape[0] // 2
    bit = (lax.axis_index(axis) // distance) % 2
    given = lax.dynamic_slice_in_dim(kept, (1 - bit) * half, half, 0).astype(jnp.bfloat16)
    return lax.dynamic_slice_in_dim(kept, bit * half, half, 0), given


def exchange(kept, given, axis, distance, after=None):
    taken = lax.ppermute(given, axis, swap_pairs(lax.axis_size(axis), distance))
    if after is not None:
        taken, _ = lax.optimization_barrier((taken, after))
    return kept + taken.astype(jnp.float32)


def first_halving(kept, given, order):
    kept = exchange(kept, given, *order[0])
    return halve(kept, *order[1])


def reduce_shares(chains, orders):
    chains = list(chains)
    for step in range(len(orders[0])):
        for n, order in enumerate(orders):
            after = chains[n - 1][1] if len(chains) > 1 else None
            kept = exchange(*chains[n], *order[step], after)
            last = step + 1 == len(order)
            chains[n] = (kept, None) if last else halve(kept, *order[step + 1])
    return [kept for kept, _ in chains]


class Plan:
    def __init__(self, inline_count, tile_count, inline_cells, depth_cells, chans, shares):
        self.inline_count, self.inline_cells = (inline_count, inline_cells)
        self.depth_cells = depth_cells
        self.inline_total = inline_count * inline_cells
        self.depth_total = tile_count * depth_cells
        self.chans = chans
        self.whole = inline_count == 2 and depth_cells % inline_count == 0
        self.own_depth = depth_cells // inline_count if self.whole else depth_cells
        own = range(self.own_depth)
        spread = lambda cells, d: sorted({z + d * b for z in cells for b in (-1, 0, 1)})
        self.z = {"own": list(own)}
        self.z["second"] = spread(self.z["own"], D2)
        self.z["first"] = spread(self.z["second"], D2)
        self.depth_width = depth_cells + 2 * REACH
        self.partner_reach = REACH
        self.z["near1"] = spread(self.z["own"], D1)
        self.z["near2"] = self.z["second"]
        self.z["middle"] = self.z["own"]
        reach = {"own": 0, "second": D2, "first": 2 * D2, "input": REACH, "near1": D1, "near2": D2}
        reach["middle"] = D2
        self.x = {}
        for name, halo in reach.items():
            if self.whole:
                self.x[name] = (0, self.inline_total)
            else:
                self.x[name] = (-halo, inline_cells + halo)
        self.aligned = chans % shares == 0 and inline_count % 2 == 0
        self.groups = shares if self.aligned else chans
        self.per_group = chans // self.groups
        self.pitch = 28 if self.aligned else 32
        self.rows = round_up(self.per_group * self.pitch, 8)

    def planes(self, name):
        low, high = self.x[name]
        return (high - low) * (self.depth_width if name == "input" else len(self.z[name]))

    def index(self, name, x, z):
        if name == "input":
            start = lax.axis_index("inline") * self.own_depth if self.whole else 0
            return (x - self.x[name][0]) * self.depth_width + z + start + REACH
        return (x - self.x[name][0]) * len(self.z[name]) + self.z[name].index(z)

    def runs(self, name, step):
        low, high = self.x[name]
        found = []
        for x in range(low, high):
            if self.whole:
                taps = tuple(a for a in (-1, 0, 1) if 0 <= x + step * a < self.inline_total)
            else:
                taps = (-1, 0, 1)
            if found and found[-1][0] == taps:
                found[-1][2] += 1
            else:
                found.append([taps, x, 1])
        return found


def depth_base(plan):
    start = lax.axis_index("tile") * plan.depth_cells
    if plan.whole:
        start = start + lax.axis_index("inline") * plan.own_depth
    return start


def inside(plan, x, z):
    depth = depth_base(plan) + z
    good = (depth >= 0) & (depth < plan.depth_total)
    if not plan.whole:
        cell = lax.axis_index("inline") * plan.inline_cells + x
        good = good & (cell >= 0) & (cell < plan.inline_total)
    return good


def each(count, body, unrolled=4):
    if count <= unrolled:
        for i in range(count):
            body(i)
    else:
        lax.fori_loop(0, count, lambda i, carry: (body(i), carry)[1], 0)


def shifted(plane, amount):
    if amount == 0:
        return plane
    width = plane.shape[1]
    column = lax.broadcasted_iota(jnp.int32, plane.shape, 1) + amount
    rolled = pltpu.roll(plane, (-amount) % width, 1)
    return jnp.where((column >= 0) & (column < width), rolled, 0.0)


def store_taps(ref, index, plane, offsets):
    chans = plane.shape[0]
    for place, amount in enumerate(offsets):
        ref[index, place * chans : (place + 1) * chans, :] = shifted(plane, amount).astype(
            jnp.bfloat16
        )


def sigmoid(value):
    return 1.0 / (1.0 + jnp.exp(-value))


def slope_of(value, sig):
    return sig * (1.0 + value * (1.0 - sig))


def matmul(left, right):
    return lax.dot_general(
        left, right, (((1,), (0,)), ((), ())), preferred_element_type=jnp.float32
    )


def matmul_nt(left, right):
    return lax.dot_general(
        left, right, (((1,), (1,)), ((), ())), preferred_element_type=jnp.float32
    )


def conv(weight_ref, taps, columns):
    total = None
    for a in taps:
        term = matmul(weight_ref[a + 1], columns(a))
        total = term if total is None else total + term
    return total


def joined(pieces, axis):
    return pieces[0] if len(pieces) == 1 else jnp.concatenate(pieces, axis=axis)


def softmax_cot(raw, expo, slope, label, scale):
    count = len(raw)
    total = expo[0]
    for n in range(1, count):
        total = total + expo[n]
    found = []
    for n in range(count):
        hit = jnp.where(label == float(n), 1.0, 0.0)
        found.append((expo[n] / total - hit) * slope[n] * scale)
    return found


def load_planes(plan, planes_refs, input_ref, marks_ref):
    chans = plan.chans

    def load(ref, i, to):
        plane = ref[i, :chans, :].astype(jnp.float32)
        store_taps(input_ref, to, plane, (-D1, 0, D1))
        marks_ref[to] = ref[i, chans : chans + LABEL_ROWS, :].astype(jnp.float32)

    if not plan.whole:
        (ref,) = planes_refs
        each(plan.planes("input"), lambda i: load(ref, i, i))
        return
    here = lax.axis_index("inline")
    width = plan.depth_width
    lower = lambda k: REACH - 1 - k
    upper = lambda k: REACH + plan.depth_cells + k
    for ref, fetcher, cells, place in (
        (planes_refs[0], here, plan.depth_cells, lambda k: REACH + k),
        (planes_refs[1], here, REACH, lambda k: jnp.where(here == 0, lower(k), upper(k))),
        (planes_refs[2], 1 - here, plan.partner_reach, lambda k: jnp.where(here == 0, upper(k), lower(k))),
    ):

        def row(i, ref=ref, fetcher=fetcher, cells=cells, place=place):
            x = lax.rem(i + fetcher * plan.inline_cells, plan.inline_total)
            for k in range(cells):
                load(ref, i * cells + k, x * width + place(k))

        each(plan.inline_total, row, 1)


def forward_kernel(plan, classes, scale, *refs):
    count = 3 if plan.whole else 1
    planes_refs, refs = (refs[:count], refs[count:])
    (
        w1_ref,
        w2_ref,
        rows_ref,
        cols_ref,
        near1_ref,
        near2_ref,
        slope1_ref,
        slope2_ref,
        delta_ref,
        cot_ref,
        stats_ref,
        sums_ref,
        input_ref,
        first_ref,
        base_ref,
        marks_ref,
    ) = refs
    chans = plan.chans
    faults, horizons, salts = classes
    zs = plan.z
    load_planes(plan, planes_refs, input_ref, marks_ref)

    for taps, begin, count in plan.runs("first", D1):

        def first(i, taps=taps, begin=begin):
            x = begin + i

            def columns(a):
                return joined(
                    [
                        joined(
                            [
                                input_ref[plan.index("input", x + D1 * a, z + D1 * b)]
                                for b in (-1, 0, 1)
                            ],
                            0,
                        )
                        for z in zs["first"]
                    ],
                    1,
                )

            pre = conv(w1_ref, taps, columns)
            for j, z in enumerate(zs["first"]):
                value = pre[:, j * 128 : (j + 1) * 128]
                field = input_ref[plan.index("input", x, z), chans : 2 * chans, :]
                sig = sigmoid(value)
                out = field.astype(jnp.float32) + value * sig
                out = out.astype(jnp.bfloat16).astype(jnp.float32)
                out = jnp.where(inside(plan, x, z), out, 0.0)
                store_taps(first_ref, plan.index("first", x, z), out, (-D2, 0, D2))
                if z in zs["own"]:
                    base_ref[plan.index("first", x, z)] = slope_of(value, sig)

        each(count, first)

    own_low, own_high = plan.x["own"]

    def keep_slope(i):
        x = own_low + i
        for z in zs["own"]:
            slope1_ref[plan.index("own", x, z)] = base_ref[plan.index("first", x, z)]

    each(own_high - own_low, keep_slope)

    for name, ref, source, source_ref in (
        ("near1", near1_ref, "input", input_ref),
        ("near2", near2_ref, "first", first_ref),
    ):
        near_low, near_high = plan.x[name]

        def keep(i, name=name, ref=ref, source=source, source_ref=source_ref, near_low=near_low):
            x = near_low + i
            for z in zs[name]:
                ref[plan.index(name, x, z)] = source_ref[plan.index(source, x, z)]

        each(near_high - near_low, keep)

    spread = [
        jnp.broadcast_to(cols_ref[:, n : n + 1], (chans, 128)) for n in range(faults + horizons)
    ]
    for n in range(faults + horizons):
        base_ref[n] = spread[n]

    used = (plan.x["second"][1] - plan.x["second"][0]) * (1 + salts)
    if used < sums_ref.shape[0]:
        sums_ref[used:, :] = jnp.zeros((sums_ref.shape[0] - used, 128), jnp.float32)

    for taps, begin, count in plan.runs("second", D2):

        def second(i, taps=taps, begin=begin):
            x = begin + i

            def columns(a):
                return joined(
                    [
                        joined(
                            [
                                first_ref[plan.index("first", x + D2 * a, z + D2 * b)]
                                for b in (-1, 0, 1)
                            ],
                            0,
                        )
                        for z in zs["second"]
                    ],
                    1,
                )

            pre = conv(w2_ref, taps, columns)
            field = joined(
                [
                    first_ref[plan.index("first", x, z), chans : 2 * chans, :]
                    for z in zs["second"]
                ],
                1,
            )
            sig = sigmoid(pre)
            slope2 = slope_of(pre, sig)
            second_out = (field.astype(jnp.float32) + pre * sig).astype(jnp.bfloat16)
            raw = matmul(rows_ref[...], second_out)
            squash = jnp.tanh(raw / CAPPING)
            expo = jnp.exp(CAPPING * squash)
            slope = 1.0 - squash * squash
            sums = None
            for j, z in enumerate(zs["second"]):
                lanes = slice(j * 128, (j + 1) * 128)
                row = lambda table, n: table[n : n + 1, lanes]
                marks = marks_ref[plan.index("input", x, z)]
                good = inside(plan, x, z)
                here = plan.index("second", x, z)
                slope2_ref[here] = slope2[:, lanes]
                for task, start, size in ((0, 0, faults), (1, faults, horizons)):
                    span = range(start, start + size)
                    dlog = softmax_cot(
                        [row(raw, n) for n in span],
                        [row(expo, n) for n in span],
                        [row(slope, n) for n in span],
                        marks[task : task + 1, :],
                        scale,
                    )
                    cot = None
                    for n, factor in zip(span, dlog):
                        term = base_ref[n] * factor
                        cot = term if cot is None else cot + term
                    if z in zs["own"]:
                        cot_ref[task, plan.index("middle", x, z)] = cot
                    delta = jnp.where(good, cot * slope2[:, lanes], 0.0)
                    delta_ref[task, here] = delta.astype(jnp.bfloat16)
                query = faults + horizons
                pieces = [row(expo, query)]
                pieces += [row(raw, query + 1 + n) for n in range(salts)]
                pieces += [row(slope, query), marks[2:3, :]]
                for n, piece in enumerate(pieces):
                    stats_ref[here, n : n + 1, :] = piece
                if z in zs["own"]:
                    terms = [pieces[0]] + [pieces[0] * piece for piece in pieces[1 : 1 + salts]]
                    if sums is None:
                        sums = terms
                    else:
                        sums = [old + new for old, new in zip(sums, terms)]
            place = x - plan.x["second"][0]
            for n, piece in enumerate(sums):
                sums_ref[pl.ds(place * (1 + salts) + n, 1), :] = piece

        each(count, second)


def salt_cotangents(plan, classes, scale, stats_ref, sums_ref, cols_ref, slope2_ref, delta_ref, cot_ref, spread_ref):
    faults, horizons, salts = classes
    chans = plan.chans
    query = faults + horizons
    for n in range(salts + 1):
        spread_ref[n] = jnp.broadcast_to(cols_ref[:, query + n : query + n + 1], (chans, 128))
    low, high = plan.x["second"]

    def one(i):
        x = low + i
        sums = [sums_ref[pl.ds(i * (1 + salts) + n, 1), :] for n in range(1 + salts)]
        total = sums[0]
        salt_raw = [value / total for value in sums[1:]]
        squash = [jnp.tanh(value / CAPPING) for value in salt_raw]
        label = stats_ref[plan.index("second", x, 0), salts + 2 : salts + 3, :]
        dlog = softmax_cot(
            salt_raw,
            [jnp.exp(CAPPING * value) for value in squash],
            [1.0 - value * value for value in squash],
            label,
            scale,
        )
        inner = dlog[0] * salt_raw[0]
        for n in range(1, salts):
            inner = inner + dlog[n] * salt_raw[n]
        for z in plan.z["second"]:
            here = plan.index("second", x, z)
            attn = stats_ref[here, 0:1, :] / total
            along = dlog[0] * stats_ref[here, 1:2, :]
            for n in range(1, salts):
                along = along + dlog[n] * stats_ref[here, 1 + n : 2 + n, :]
            dscore = attn * (along - inner) * stats_ref[here, salts + 1 : salts + 2, :]
            cot = spread_ref[0] * dscore
            for n in range(salts):
                cot = cot + spread_ref[1 + n] * (attn * dlog[n])
            cot_ref[0, here] = cot
            delta = jnp.where(inside(plan, x, z), cot * slope2_ref[here], 0.0)
            delta_ref[0, here] = delta.astype(jnp.bfloat16)

    each(high - low, one)


def backward_body(
    plan,
    tasks,
    delta_ref,
    cot_of,
    slope1_ref,
    near1_ref,
    near2_ref,
    w2t_ref,
    outs,
    taps_ref,
    first_delta_ref,
    second_delta_ref,
    rows_refs,
    slots,
):
    chans, zs = (plan.chans, plan.z)
    width = tasks * chans

    def spread(i):
        for task in range(tasks):
            plane = delta_ref[task, i].astype(jnp.float32)
            store_taps(taps_ref, task * plan.planes("second") + i, plane, (D2, 0, -D2))

    each(plan.planes("second"), spread)

    for taps, begin, count in plan.runs("own", -D2):

        def back(i, taps=taps, begin=begin):
            x = begin + i

            def columns(a):
                return joined(
                    [
                        joined(
                            [
                                taps_ref[
                                    task * plan.planes("second")
                                    + plan.index("second", x - D2 * a, z - D2 * b)
                                ]
                                for b in (-1, 0, 1)
                            ],
                            0,
                        )
                        for task in range(tasks)
                        for z in zs["own"]
                    ],
                    1,
                )

            pulled = conv(w2t_ref, taps, columns)
            column = 0
            for task in range(tasks):
                for z in zs["own"]:
                    here = plan.index("own", x, z)
                    cot = cot_of(task, x, z) + pulled[:, column * 128 : (column + 1) * 128]
                    place = slice(task * chans, (task + 1) * chans)
                    first_delta_ref[here, place, :] = (cot * slope1_ref[here]).astype(jnp.bfloat16)
                    second_delta_ref[here, place, :] = delta_ref[task, plan.index("second", x, z)]
                    column += 1

        each(count, back)

    own_low, own_high = plan.x["own"]
    lanes = 128
    for ref in rows_refs:
        ref[chans * plan.pitch :, :] = jnp.zeros((8, lanes), jnp.float32)
    for tap in range(27, plan.pitch):
        for ref in rows_refs:
            ref[pl.ds(tap, chans, stride=plan.pitch), :] = jnp.zeros((chans, lanes), jnp.float32)
    for a in (-1, 0, 1):
        for b in (-1, 0, 1):
            chunks = {}
            for ref, name, d, delta_own, begin in (
                (near1_ref, "near1", D1, first_delta_ref, 0),
                (near2_ref, "near2", D2, second_delta_ref, width),
            ):
                cells = []
                for x in range(own_low, own_high):
                    if plan.whole and not 0 <= x + d * a < plan.inline_total:
                        continue
                    cells += [(x, z) for z in zs["own"]]
                left = joined([ref[plan.index(name, x + d * a, z + d * b)] for x, z in cells], 1)
                right = joined([delta_own[plan.index("own", x, z)] for x, z in cells], 1)
                before = begin % lanes
                after = -(before + width) % lanes
                parts = [right]
                if before:
                    parts = [jnp.zeros((before, right.shape[1]), right.dtype)] + parts
                if after:
                    parts = parts + [jnp.zeros((after, right.shape[1]), right.dtype)]
                grad = matmul_nt(left, joined(parts, 0))
                for n in range(grad.shape[1] // lanes):
                    chunk = begin // lanes + n
                    piece = grad[:, n * lanes : (n + 1) * lanes]
                    chunks[chunk] = chunks[chunk] + piece if chunk in chunks else piece
            for chunk, value in chunks.items():
                for c in range(3):
                    tap = 9 * (a + 1) + 3 * (b + 1) + c
                    rows_refs[chunk][pl.ds(tap, chans, stride=plan.pitch), :] = value[
                        c * chans : (c + 1) * chans, :
                    ]
    if plan.aligned:
        kept_ref, given_ref = outs
        half = lax.rem(lax.axis_index("inline"), 2)
        tiles = plan.groups // plan.inline_count
        length = plan.per_group * plan.pitch
        for high in range(plan.inline_count // 2):
            for chunk, ref in enumerate(rows_refs):
                span = slice(chunk * lanes, (chunk + 1) * lanes)
                for target_ref, bit in ((kept_ref, half), (given_ref, 1 - half)):
                    start = pl.multiple_of((2 * high + bit) * tiles * length, 8)
                    block = ref.at[pl.ds(start, tiles * length + 8), :]
                    for j in range(tiles):
                        value = block[j * length : j * length + plan.rows, :]
                        target_ref[slots[high * tiles + j], :, span] = value.astype(
                            target_ref.dtype
                        )
    else:
        (out_ref,) = outs

        def write(j):
            for chunk, ref in enumerate(rows_refs):
                start = pl.multiple_of(j * plan.pitch, 8)
                span = slice(chunk * lanes, (chunk + 1) * lanes)
                out_ref[j, :, span] = ref[pl.ds(start, plan.pitch), :]

        each(plan.groups, write)


def pair_kernel(
    plan, slots, delta_ref, cot_ref, slope1_ref, near1_ref, near2_ref, w2t_ref, *rest
):
    outs, scratch = split_refs(plan, rest)
    cot_of = lambda task, x, z: cot_ref[task, plan.index("middle", x, z)]
    backward_body(
        plan,
        2,
        delta_ref,
        cot_of,
        slope1_ref,
        near1_ref,
        near2_ref,
        w2t_ref,
        outs,
        *scratch[:3],
        scratch[3:],
        slots,
    )


def salt_kernel(
    plan,
    slots,
    classes,
    scale,
    stats_ref,
    sums_ref,
    cols_ref,
    slope2_ref,
    slope1_ref,
    near1_ref,
    near2_ref,
    w2t_ref,
    *rest,
):
    outs, scratch = split_refs(plan, rest)
    delta_ref, cot_ref, spread_ref = scratch[:3]
    salt_cotangents(
        plan,
        classes,
        scale,
        stats_ref,
        sums_ref,
        cols_ref,
        slope2_ref,
        delta_ref,
        cot_ref,
        spread_ref,
    )
    cot_of = lambda task, x, z: cot_ref[task, plan.index("second", x, z)]
    backward_body(
        plan,
        1,
        delta_ref,
        cot_of,
        slope1_ref,
        near1_ref,
        near2_ref,
        w2t_ref,
        outs,
        *scratch[3:6],
        scratch[6:],
        slots,
    )


def split_refs(plan, refs):
    count = 2 if plan.aligned else 1
    return (refs[:count], refs[count:])


def vmem(count):
    return [pl.BlockSpec(memory_space=pltpu.VMEM)] * count


def backward_shapes(plan, tasks):
    chans = plan.chans
    width = round_up(2 * tasks * chans, 128)
    if plan.aligned:
        shape = (plan.groups // 2, plan.rows, width)
        outs = [jax.ShapeDtypeStruct(shape, jnp.float32), jax.ShapeDtypeStruct(shape, jnp.bfloat16)]
    else:
        outs = [jax.ShapeDtypeStruct((plan.groups, plan.pitch, width), jnp.float32)]
    scratch = [
        pltpu.VMEM((tasks * plan.planes("second"), 3 * chans, 128), jnp.bfloat16),
        pltpu.VMEM((plan.planes("own"), tasks * chans, 128), jnp.bfloat16),
        pltpu.VMEM((plan.planes("own"), tasks * chans, 128), jnp.bfloat16),
    ]
    scratch += [pltpu.VMEM((chans * plan.pitch + 8, 128), jnp.float32)] * (width // 128)
    return (outs, scratch)


def tap_major(weight, flip):
    ins, _, outs = weight.shape
    parts = weight.reshape(ins, 3, 9, outs)
    if flip:
        parts = parts.transpose(1, 0, 2, 3).reshape(3, ins, 9 * outs)
    else:
        parts = parts.transpose(1, 3, 2, 0).reshape(3, outs, 9 * ins)
    return with_layout_constraint(parts, Layout(major_to_minor=(0, 1, 2)))


def slots_of(plan, order):
    if not plan.aligned:
        return None
    tiles = plan.groups // plan.inline_count
    slots = []
    for high in range(plan.inline_count // 2):
        for tile in range(tiles):
            slot = 0
            for axis, distance in order[1:]:
                index = 2 * high if axis == "inline" else tile
                slot = 2 * slot + index // distance % 2
            slots.append(slot)
    return slots


def on_device(
    features,
    conv1_weight,
    conv2_weight,
    fault_head,
    horizon_head,
    salt_query,
    salt_head,
    fault_labels,
    horizon_labels,
    salt_labels,
):
    chans, inline_cells, depth_cells, cross_cells = features.shape
    inline_count, tile_count = (lax.axis_size("inline"), lax.axis_size("tile"))
    shares = inline_count * tile_count
    plan = Plan(inline_count, tile_count, inline_cells, depth_cells, chans, shares)
    scale = 1.0 / math.sqrt(plan.inline_total * plan.depth_total * cross_cells)
    classes = (fault_head.shape[1], horizon_head.shape[1], salt_head.shape[1])

    marks = jnp.stack(
        [
            fault_labels,
            horizon_labels,
            jnp.broadcast_to(salt_labels[:, None, :], fault_labels.shape),
        ],
        axis=2,
    ).astype(jnp.bfloat16)
    marks = jnp.pad(marks, ((0, 0), (0, 0), (0, LABEL_ROWS - 3), (0, 0)))
    planes = jnp.concatenate([features.transpose(1, 2, 0, 3), marks], axis=2)
    cols = jnp.concatenate([fault_head, horizon_head, salt_query[:, None], salt_head], axis=1)
    cols = jnp.pad(cols, ((0, 0), (0, 16 - cols.shape[1])))
    riders = [
        [cols.T, cols.astype(jnp.float32), tap_major(conv1_weight, False)],
        [tap_major(conv2_weight, False), tap_major(conv2_weight, True)],
    ]
    if plan.whole:
        other = lax.ppermute(planes, "inline", [(0, 1), (1, 0)])
        planes = jnp.concatenate([planes, other], axis=0)
        mine, theirs, riders = outward(planes, REACH, plan.partner_reach, riders)
        sources = [planes, mine, theirs]
    else:
        planes = window(planes, "tile", 1, REACH)
        sources = [window(planes, "inline", 0, REACH)]
        riders = riders[0] + riders[1]
    sources = [source.reshape((-1,) + source.shape[2:]) for source in sources]
    rows, cols, w1, w2, w2t = riders

    f32, bf16 = (jnp.float32, jnp.bfloat16)
    own, second = (plan.planes("own"), plan.planes("second"))
    second_x = plan.x["second"][1] - plan.x["second"][0]
    shape = jax.ShapeDtypeStruct
    near1, near2, slope1, slope2, delta, cot, stats, sums = pl.pallas_call(
        functools.partial(forward_kernel, plan, classes, scale),
        out_shape=[
            shape((plan.planes("near1"), 3 * chans, 128), bf16),
            shape((plan.planes("near2"), 3 * chans, 128), bf16),
            shape((own, chans, 128), f32),
            shape((second, chans, 128), f32),
            shape((2, second, chans, 128), bf16),
            shape((2, plan.planes("middle"), chans, 128), f32),
            shape((second, 8, 128), f32),
            shape((round_up(second_x * (1 + classes[2]), 8), 128), f32),
        ],
        in_specs=vmem(len(sources) + 4),
        out_specs=vmem(8),
        scratch_shapes=[
            pltpu.VMEM((plan.planes("input"), 3 * chans, 128), bf16),
            pltpu.VMEM((plan.planes("first"), 3 * chans, 128), bf16),
            pltpu.VMEM((plan.planes("first"), chans, 128), f32),
            pltpu.VMEM((plan.planes("input"), LABEL_ROWS, 128), f32),
        ],
        name="forward",
    )(*sources, w1, w2, rows, cols)

    sums = share_sums(sums, AXES if plan.whole else ("tile",))

    orders = [halving_order(0), halving_order(len(bits(tile_count)) // 2)]
    outs, scratch = backward_shapes(plan, 2)
    pair = pl.pallas_call(
        functools.partial(pair_kernel, plan, slots_of(plan, orders[0])),
        out_shape=outs,
        in_specs=vmem(6),
        out_specs=vmem(len(outs)),
        scratch_shapes=scratch,
        name="pair",
    )(delta, cot, slope1, near1, near2, w2t)
    if plan.aligned:
        pair = first_halving(*pair, orders[0])
    sums, *pair = lax.optimization_barrier((sums, *pair))
    outs, scratch = backward_shapes(plan, 1)
    scratch = [
        pltpu.VMEM((1, second, chans, 128), bf16),
        pltpu.VMEM((1, second, chans, 128), f32),
        pltpu.VMEM((1 + classes[2], chans, 128), f32),
    ] + scratch
    salt = pl.pallas_call(
        functools.partial(
            salt_kernel, plan, slots_of(plan, orders[1]), classes, plan.depth_total * scale
        ),
        out_shape=outs,
        in_specs=vmem(8),
        out_specs=vmem(len(outs)),
        scratch_shapes=scratch,
        name="salt",
    )(stats, sums, cols, slope2, slope1, near1, near2, w2t)

    terms = []
    if plan.aligned:
        salt = first_halving(*salt, orders[1])
        shared = reduce_shares([pair, salt], [order[1:] for order in orders])
        for share, tasks in zip(shared, (2, 1)):
            share = share[0, : plan.per_group * plan.pitch]
            share = share.reshape(plan.per_group, plan.pitch, -1)
            share = share[:, :27, : 2 * tasks * chans].reshape(-1, 2, tasks, chans)
            terms.append(share.transpose(1, 2, 0, 3).reshape(2, tasks, -1))
        grads = jnp.concatenate(terms, axis=1)
    else:
        for (value,), tasks in ((pair, 2), (salt, 1)):
            value = value[:, :27, : 2 * tasks * chans].reshape(chans, 27, 2, tasks, chans)
            terms.append(value.transpose(2, 3, 0, 1, 4).reshape(2, tasks, shares, -1))
        flat = jnp.concatenate(terms, axis=1).transpose(2, 0, 1, 3)
        left = [(axis, d) for axis in AXES for d in reversed(bits(lax.axis_size(axis)))]
        flat = flat.reshape((2,) * len(left) + flat.shape[1:])
        places = [left.index(entry) for entry in orders[0]]
        flat = flat.transpose(places + [len(left), len(left) + 1, len(left) + 2])
        flat = flat.reshape((-1,) + flat.shape[len(left) :])
        grads = reduce_shares([halve(flat, *orders[0][0])], orders[:1])[0][0]
    gram = jnp.sum(grads[:, :, None, :] * grads[:, None, :, :], axis=3)
    gram = share_sums(gram.reshape(2, 9), AXES).reshape(2, 3, 3) / (27 * chans * chans)
    return (grads, gram)


def solution(mesh):
    in_specs = (
        P(None, "inline", "tile", None),
        P(),
        P(),
        P(),
        P(),
        P(),
        P(),
        P("inline", "tile", None),
        P("inline", "tile", None),
        P("inline", None),
    )
    out_specs = (P(None, None, ("inline", "tile")), P())
    return jax.shard_map(
        on_device, mesh=mesh, in_specs=in_specs, out_specs=out_specs, check_vma=False
    )
```

profile of v0, /device:TPU:0, one launch (start us, length us, event | category | flops | bytes accessed | tf_op | source)
XLA Modules:
  0.0 116.4 jit_solution(6217265947515873588)
XLA Ops:
  0.6 0.7 convert.14
  1.4 0.7 convert_bitcast_fusion
  2.1 0.9 copy.149
  3.6 1.0 collective-permute-done
  4.7 4.7 %collective-permute-start.1 = (bf16[4,2,104,128]{3,2,1,0:T(8,128)(2,1)S(1)}, bf16[4,2,104,128]{3,2,1,0:T(8,128)(2,1)S(1)}, u32[]{:S(2)}, u32[]{:S(2)}) collective-permute-start(bf16[4,2,104,128]{3,2,1,0:T(8,128)(2,1)S(1)} %reverse_select_fusion), channel_id=1, source_target_pairs={{0,1},{1,2},{2,3},{3,4},{4,5},{5,6},{6,7},{7,8},{8,9},{9,10},{10,1... | collective-permute-start | bytes 638984 | tf_op jit(solution)/shard_map/ppermute | solution.py:63
  9.4 0.7 pad_maximum_fusion.4
  10.3 1.1 copy.128.refs_3_
  11.4 0.6 pad_convert_fusion
  12.0 3.1 %collective-permute-done.1 = bf16[4,2,104,128]{3,2,1,0:T(8,128)(2,1)S(1)} collective-permute-done((bf16[4,2,104,128]{3,2,1,0:T(8,128)(2,1)S(1)}, bf16[4,2,104,128]{3,2,1,0:T(8,128)(2,1)S(1)}, u32[]{:S(2)}, u32[]{:S(2)}) %collective-permute-start.1) | collective-permute-done | bytes 213024 | tf_op jit(solution)/shard_map/ppermute | solution.py:63
  15.1 3.3 %collective-permute-start.2 = (bf16[4,3,104,128]{3,2,1,0:T(8,128)(2,1)S(1)}, bf16[4,3,104,128]{3,2,1,0:T(8,128)(2,1)S(1)}, u32[]{:S(2)}, u32[]{:S(2)}) collective-permute-start(bf16[4,3,104,128]{3,2,1,0:T(8,128)(2,1)S(1)} %pad_maximum_fusion), channel_id=1, source_target_pairs={{0,2},{1,3},{2,4},{3,5},{4,6},{5,7},{6,8},{7,9},{8,10},{9,11},{10,... | collective-permute-start | bytes 958472 | tf_op jit(solution)/shard_map/ppermute | solution.py:63
  18.7 1.1 copy.131.w2t_ref
  19.8 1.1 copy.129.refs_4_
  20.9 3.8 %collective-permute-done.2 = bf16[4,3,104,128]{3,2,1,0:T(8,128)(2,1)S(1)} collective-permute-done((bf16[4,3,104,128]{3,2,1,0:T(8,128)(2,1)S(1)}, bf16[4,3,104,128]{3,2,1,0:T(8,128)(2,1)S(1)}, u32[]{:S(2)}, u32[]{:S(2)}) %collective-permute-start.2) | collective-permute-done | bytes 319520 | tf_op jit(solution)/shard_map/ppermute | solution.py:63
  24.8 0.7 copy.132.refs_5_
  25.6 1.2 %collective-permute-done.3 = bf16[4,5,104,128]{3,2,1,0:T(8,128)(2,1)S(1)} collective-permute-done((bf16[4,5,104,128]{3,2,1,0:T(8,128)(2,1)S(1)}, bf16[4,5,104,128]{3,2,1,0:T(8,128)(2,1)S(1)}, u32[]{:S(2)}, u32[]{:S(2)}) %collective-permute-start.3) | collective-permute-done | bytes 532512 | tf_op jit(solution)/shard_map/ppermute | solution.py:73
  26.8 0.8 copy-done.5
  27.5 8.3 %forward.1 = (bf16[12,288,128]{2,1,0:T(8,128)(2,1)}, bf16[12,288,128]{2,1,0:T(8,128)(2,1)}, f32[4,96,128]{2,1,0:T(8,128)}, f32[12,96,128]{2,1,0:T(8,128)}, bf16[...) custom-call(bf16[8,104,128]{2,1,0:T(8,128)(2,1)} %bitcast.39, ...), custom_call_target="tpu_custom_call" | custom-call | tf_op jit(solution)/shard_map/forward/pallas_call | solution.py:804
  35.9 7.1 %pair.1 = (f32[16,88,384]{2,1,0:T(8,128)}, bf16[16,88,384]{2,1,0:T(8,128)(2,1)}) custom-call(bf16[2,12,96,128]{3,2,1,0:T(8,128)(2,1)} %get-tuple-element.38.delta_ref, f32[2,4,96,128]{3,2,1,0:T(8,128)} %get-tuple-element.39.cot_ref, f32[4,96,128]{2,1,0:T(8,128)} %get-tuple-element.40.slope1_ref, bf16[12,288,128]{2,1,0:T(8,128)(2,1)} %get-tuple-element.41.near1_ref, ...), custom_call_target="tpu_custom_call" | custom-call | tf_op jit(solution)/shard_map/pair/pallas_call | solution.py:831
  43.2 0.7 broadcast_in_dim.13
  43.9 7.2 %all-to-all-start = ((f32[32,16,128]{2,1,0:T(8,128)}), f32[32,16,128]{2,1,0:T(8,128)S(1)}, u32[]{:S(2)}, u32[]{:S(2)}) async-start(f32[32,16,128]{2,1,0:T(8,128)} %broadcast_in_dim.13), calls=%async_computation | async-start | bytes 524288 | tf_op jit(solution)/shard_map/all_to_all | solution.py:79
  51.1 11.0 %all-to-all-done = f32[32,16,128]{2,1,0:T(8,128)S(1)} async-done(((f32[32,16,128]{2,1,0:T(8,128)}), f32[32,16,128]{2,1,0:T(8,128)S(1)}, u32[]{:S(2)}, u32[]{:S(2)}) %all-to-all-start) | async-done | bytes 262176 | tf_op jit(solution)/shard_map/all_to_all | solution.py:79
  62.7 1.8 %convert_add_fusion = f32[16,88,384]{2,1,0:T(8,128)S(1)} fusion(f32[16,88,384]{2,1,0:T(8,128)} %get-tuple-element.44, bf16[16,88,384]{2,1,0:T(8,128)(2,1)S(1)} %collective-permute-done.4), kind=kLoop, calls=%fused_computation | loop fusion | flops 1081344 | bytes 5406720 | tf_op jit(solution)/shard_map/add | solution.py:100
  64.7 6.3 %salt.1 = (f32[16,88,256]{2,1,0:T(8,128)}, bf16[16,88,256]{2,1,0:T(8,128)(2,1)}) custom-call(f32[12,8,128]{2,1,0:T(8,128)} %get-tuple-element.48.stats_ref, f32[16,128]{1,0:T(8,128)} %reduce_sum.27.sums_ref, f32[96,16]{1,0:T(8,128)} %get-tuple-element.36.refs_6_.cols_ref, f32[12,96,128]{2,1,0:T(8,128)} %get-tuple-element.50.slope2_ref, ...), custom_call_target="tpu_custom_call" | custom-call | tf_op jit(solution)/shard_map/salt/pallas_call | solution.py:848
  71.3 2.1 %collective-permute-done.6 = bf16[16,88,256]{2,1,0:T(8,128)(2,1)S(1)} collective-permute-done((bf16[16,88,256]{2,1,0:T(8,128)(2,1)}, bf16[16,88,256]{2,1,0:T(8,128)(2,1)S(1)}, u32[]{:S(2)}, u32[]{:S(2)}) %collective-permute-start.6) | collective-permute-done | bytes 720928 | tf_op jit(solution)/shard_map/ppermute | solution.py:97
  73.4 1.5 %convert_add_fusion.1 = f32[16,88,256]{2,1,0:T(8,128)S(1)} fusion(f32[16,88,256]{2,1,0:T(8,128)} %get-tuple-element.51, bf16[16,88,256]{2,1,0:T(8,128)(2,1)S(1)} %collective-permute-done.6), kind=kLoop, calls=%fused_computation.1 | loop fusion | flops 720896 | bytes 3604480 | tf_op jit(solution)/shard_map/add | solution.py:100
  75.0 10.6 %collective-permute-done.5 = bf16[8,88,384]{2,1,0:T(8,128)(2,1)S(1)} collective-permute-done((bf16[8,88,384]{2,1,0:T(8,128)(2,1)S(1)}, bf16[8,88,384]{2,1,0:T(8,128)(2,1)S(1)}, u32[]{:S(2)}, u32[]{:S(2)}) %collective-permute-start.5) | collective-permute-done | bytes 540704 | tf_op jit(solution)/shard_map/ppermute | solution.py:97
  86.2 0.9 collective-permute-start.10
  87.1 6.8 %collective-permute-done.7 = bf16[4,88,384]{2,1,0:T(8,128)(2,1)S(1)} collective-permute-done((bf16[4,88,384]{2,1,0:T(8,128)(2,1)S(1)}, bf16[4,88,384]{2,1,0:T(8,128)(2,1)S(1)}, u32[]{:S(2)}, u32[]{:S(2)}) %collective-permute-start.7) | collective-permute-done | bytes 270368 | tf_op jit(solution)/shard_map/ppermute | solution.py:97
  94.5 4.5 %collective-permute-done.9 = bf16[2,88,384]{2,1,0:T(8,128)(2,1)S(1)} collective-permute-done((bf16[2,88,384]{2,1,0:T(8,128)(2,1)S(1)}, bf16[2,88,384]{2,1,0:T(8,128)(2,1)S(1)}, u32[]{:S(2)}, u32[]{:S(2)}) %collective-permute-start.9) | collective-permute-done | bytes 135200 | tf_op jit(solution)/shard_map/ppermute | solution.py:97
  99.3 3.0 %collective-permute-start.13 = (bf16[1,88,256]{2,1,0:T(8,128)(2,1)S(1)}, bf16[1,88,256]{2,1,0:T(8,128)(2,1)S(1)}, u32[]{:S(2)}, u32[]{:S(2)}) collective-permute-start(bf16[1,88,256]{2,1,0:T(8,128)(2,1)S(1)} %dynamic-slice_convert_fusion.7), channel_id=1, source_target_pairs={{0,8},{1,9},{2,10},{3,11},{4,12},{5,13},{6,14},{7,15},{8,0},{9,1},... | collective-permute-start | bytes 135176 | tf_op jit(solution)/shard_map/ppermute | solution.py:97
  102.2 2.3 %collective-permute-done.11 = bf16[1,88,384]{2,1,0:T(8,128)(2,1)S(1)} collective-permute-done((bf16[1,88,384]{2,1,0:T(8,128)(2,1)S(1)}, bf16[1,88,384]{2,1,0:T(8,128)(2,1)S(1)}, u32[]{:S(2)}, u32[]{:S(2)}) %collective-permute-start.11) | collective-permute-done | bytes 67616 | tf_op jit(solution)/shard_map/ppermute | solution.py:97
  106.6 9.0 %all_to_all.10 = f32[32,2,9]{2,1,0:T(2,128)S(1)} all-to-all(f32[32,2,9]{2,1,0:T(2,128)S(1)} %broadcast_in_dim.14), channel_id=1, replica_groups=mesh['inline'=2,'tile'=16] {'inline','tile'}, dimensions={0} | all-to-all | bytes 4608 | tf_op jit(solution)/shard_map/all_to_all | solution.py:79
  (76 shorter events, 6.6 us)
Async XLA Ops:
  0.6 9.6 %copy-start.4 = (bf16[96,27,96]{2,0,1:T(8,128)(2,1)S(1)}, bf16[96,27,96]{2,0,1:T(8,128)(2,1)}, u32[]{:S(2)}) copy-start(bf16[96,27,96]{2,0,1:T(8,128)(2,1)} %param.11) | copy-start | bytes 1492996
  3.1 1.5 %collective-permute-start = (bf16[2,2,104,128]{3,2,1,0:T(8,128)(2,1)S(1)}, bf16[2,2,104,128]{3,2,1,0:T(8,128)(2,1)S(1)}, u32[]{:S(2)}, u32[]{:S(2)}) collective-permute-start(bf16[2,2,104,128]{3,2,1,0:T(8,128)(2,1)S(1)} %pad_maximum_fusion.3), channel_id=1, source_target_pairs={{0,16},{16,0},{1,17},{17,1},{2,18},{18,2},{3,19},{19,3},{4,20},{20... | collective-permute-start | bytes 319496 | tf_op jit(solution)/shard_map/ppermute | solution.py:789
  3.6 14.8 %copy-start = (bf16[96,27,96]{2,0,1:T(8,128)(2,1)S(1)}, bf16[96,27,96]{2,0,1:T(8,128)(2,1)}, u32[]{:S(2)}) copy-start(bf16[96,27,96]{2,0,1:T(8,128)(2,1)} %param.12) | copy-start | bytes 1492996
  4.6 14.1 %copy-start.1 = (bf16[4,2,104,128]{3,2,1,0:T(8,128)(2,1)}, bf16[4,2,104,128]{3,2,1,0:T(8,128)(2,1)S(1)}, u32[]{:S(2)}) copy-start(bf16[4,2,104,128]{3,2,1,0:T(8,128)(2,1)S(1)} %pad_maximum_fusion.2) | copy-start | bytes 638980
  4.7 10.4 %collective-permute-start.1 = (bf16[4,2,104,128]{3,2,1,0:T(8,128)(2,1)S(1)}, bf16[4,2,104,128]{3,2,1,0:T(8,128)(2,1)S(1)}, u32[]{:S(2)}, u32[]{:S(2)}) collective-permute-start(bf16[4,2,104,128]{3,2,1,0:T(8,128)(2,1)S(1)} %reverse_select_fusion), channel_id=1, source_target_pairs={{0,1},{1,2},{2,3},{3,4},{4,5},{5,6},{6,7},{7,8},{8,9},{9,10},{10,1... | collective-permute-start | bytes 638984 | tf_op jit(solution)/shard_map/ppermute | solution.py:63
  15.1 9.6 %collective-permute-start.2 = (bf16[4,3,104,128]{3,2,1,0:T(8,128)(2,1)S(1)}, bf16[4,3,104,128]{3,2,1,0:T(8,128)(2,1)S(1)}, u32[]{:S(2)}, u32[]{:S(2)}) collective-permute-start(bf16[4,3,104,128]{3,2,1,0:T(8,128)(2,1)S(1)} %pad_maximum_fusion), channel_id=1, source_target_pairs={{0,2},{1,3},{2,4},{3,5},{4,6},{5,7},{6,8},{7,9},{8,10},{9,11},{10,... | collective-permute-start | bytes 958472 | tf_op jit(solution)/shard_map/ppermute | solution.py:63
  24.8 2.0 %copy-start.3 = (bf16[4,5,104,128]{3,2,1,0:T(8,128)(2,1)}, bf16[4,5,104,128]{3,2,1,0:T(8,128)(2,1)S(1)}, u32[]{:S(2)}) copy-start(bf16[4,5,104,128]{3,2,1,0:T(8,128)(2,1)S(1)} %constant_dynamic-update-slice_fusion) | copy-start | bytes 1597444
  24.8 2.0 %collective-permute-start.3 = (bf16[4,5,104,128]{3,2,1,0:T(8,128)(2,1)S(1)}, bf16[4,5,104,128]{3,2,1,0:T(8,128)(2,1)S(1)}, u32[]{:S(2)}, u32[]{:S(2)}) collective-permute-start(bf16[4,5,104,128]{3,2,1,0:T(8,128)(2,1)S(1)} %constant_dynamic-update-slice_fusion), channel_id=1, source_target_pairs={{0,16},{16,0},{1,17},{17,1},{2,18},{18,2},{3,19},{19,3},{4,20},{20... | collective-permute-start | bytes 1597448 | tf_op jit(solution)/shard_map/ppermute | solution.py:73
  26.8 0.8 copy-start.5
  35.9 7.3 %copy-start.6 = (f32[16,128]{1,0:T(8,128)S(1)}, f32[16,128]{1,0:T(8,128)}, u32[]{:S(2)}) copy-start(f32[16,128]{1,0:T(8,128)} %get-tuple-element.37) | copy-start | bytes 24580
  43.0 19.7 %collective-permute-start.4 = (bf16[16,88,384]{2,1,0:T(8,128)(2,1)}, bf16[16,88,384]{2,1,0:T(8,128)(2,1)S(1)}, u32[]{:S(2)}, u32[]{:S(2)}) collective-permute-start(bf16[16,88,384]{2,1,0:T(8,128)(2,1)} %get-tuple-element.45), channel_id=1, source_target_pairs={{0,16},{16,0},{1,17},{17,1},{2,18},{18,2},{3,19},{19,3},{4,20},{20... | collective-permute-start | bytes 3244040 | tf_op jit(solution)/shard_map/ppermute | solution.py:97
  43.9 18.2 %all-to-all-start = ((f32[32,16,128]{2,1,0:T(8,128)}), f32[32,16,128]{2,1,0:T(8,128)S(1)}, u32[]{:S(2)}, u32[]{:S(2)}) async-start(f32[32,16,128]{2,1,0:T(8,128)} %broadcast_in_dim.13), calls=%async_computation | async-start | bytes 524288 | tf_op jit(solution)/shard_map/all_to_all | solution.py:79
  71.0 2.4 %collective-permute-start.6 = (bf16[16,88,256]{2,1,0:T(8,128)(2,1)}, bf16[16,88,256]{2,1,0:T(8,128)(2,1)S(1)}, u32[]{:S(2)}, u32[]{:S(2)}) collective-permute-start(bf16[16,88,256]{2,1,0:T(8,128)(2,1)} %get-tuple-element.52), channel_id=1, source_target_pairs={{0,16},{16,0},{1,17},{17,1},{2,18},{18,2},{3,19},{19,3},{4,20},{20... | collective-permute-start | bytes 2162696 | tf_op jit(solution)/shard_map/ppermute | solution.py:97
  71.0 14.7 %collective-permute-start.5 = (bf16[8,88,384]{2,1,0:T(8,128)(2,1)S(1)}, bf16[8,88,384]{2,1,0:T(8,128)(2,1)S(1)}, u32[]{:S(2)}, u32[]{:S(2)}) collective-permute-start(bf16[8,88,384]{2,1,0:T(8,128)(2,1)S(1)} %dynamic-slice_convert_fusion), channel_id=1, source_target_pairs={{0,1},{1,0},{2,3},{3,2},{4,5},{5,4},{6,7},{7,6},{8,9},{9,8},{10,11... | collective-permute-start | bytes 1622024 | tf_op jit(solution)/shard_map/ppermute | solution.py:97
  74.9 11.1 %collective-permute-start.8 = (bf16[8,88,256]{2,1,0:T(8,128)(2,1)S(1)}, bf16[8,88,256]{2,1,0:T(8,128)(2,1)S(1)}, u32[]{:S(2)}, u32[]{:S(2)}) collective-permute-start(bf16[8,88,256]{2,1,0:T(8,128)(2,1)S(1)} %dynamic-slice_convert_fusion.1), channel_id=1, source_target_pairs={{0,4},{1,5},{2,6},{3,7},{4,0},{5,1},{6,2},{7,3},{8,12},{9,13},{10,... | collective-permute-start | bytes 1081352 | tf_op jit(solution)/shard_map/ppermute | solution.py:97
  85.8 8.1 %collective-permute-start.7 = (bf16[4,88,384]{2,1,0:T(8,128)(2,1)S(1)}, bf16[4,88,384]{2,1,0:T(8,128)(2,1)S(1)}, u32[]{:S(2)}, u32[]{:S(2)}) collective-permute-start(bf16[4,88,384]{2,1,0:T(8,128)(2,1)S(1)} %dynamic-slice_convert_fusion.2), channel_id=1, source_target_pairs={{0,2},{1,3},{2,0},{3,1},{4,6},{5,7},{6,4},{7,5},{8,10},{9,11},{10,... | collective-permute-start | bytes 811016 | tf_op jit(solution)/shard_map/ppermute | solution.py:97
  86.2 7.9 %collective-permute-start.10 = (bf16[4,88,256]{2,1,0:T(8,128)(2,1)S(1)}, bf16[4,88,256]{2,1,0:T(8,128)(2,1)S(1)}, u32[]{:S(2)}, u32[]{:S(2)}) collective-permute-start(bf16[4,88,256]{2,1,0:T(8,128)(2,1)S(1)} %dynamic-slice_convert_fusion.3), channel_id=1, source_target_pairs={{0,1},{1,0},{2,3},{3,2},{4,5},{5,4},{6,7},{7,6},{8,9},{9,8},{10,11... | collective-permute-start | bytes 540680 | tf_op jit(solution)/shard_map/ppermute | solution.py:97
  94.0 5.1 %collective-permute-start.9 = (bf16[2,88,384]{2,1,0:T(8,128)(2,1)S(1)}, bf16[2,88,384]{2,1,0:T(8,128)(2,1)S(1)}, u32[]{:S(2)}, u32[]{:S(2)}) collective-permute-start(bf16[2,88,384]{2,1,0:T(8,128)(2,1)S(1)} %dynamic-slice_convert_fusion.4), channel_id=1, source_target_pairs={{0,4},{1,5},{2,6},{3,7},{4,0},{5,1},{6,2},{7,3},{8,12},{9,13},{10,... | collective-permute-start | bytes 405512 | tf_op jit(solution)/shard_map/ppermute | solution.py:97
  94.2 5.0 %collective-permute-start.12 = (bf16[2,88,256]{2,1,0:T(8,128)(2,1)S(1)}, bf16[2,88,256]{2,1,0:T(8,128)(2,1)S(1)}, u32[]{:S(2)}, u32[]{:S(2)}) collective-permute-start(bf16[2,88,256]{2,1,0:T(8,128)(2,1)S(1)} %dynamic-slice_convert_fusion.5), channel_id=1, source_target_pairs={{0,2},{1,3},{2,0},{3,1},{4,6},{5,7},{6,4},{7,5},{8,10},{9,11},{10,... | collective-permute-start | bytes 270344 | tf_op jit(solution)/shard_map/ppermute | solution.py:97
  99.1 5.5 %collective-permute-start.11 = (bf16[1,88,384]{2,1,0:T(8,128)(2,1)S(1)}, bf16[1,88,384]{2,1,0:T(8,128)(2,1)S(1)}, u32[]{:S(2)}, u32[]{:S(2)}) collective-permute-start(bf16[1,88,384]{2,1,0:T(8,128)(2,1)S(1)} %dynamic-slice_convert_fusion.6), channel_id=1, source_target_pairs={{0,8},{1,9},{2,10},{3,11},{4,12},{5,13},{6,14},{7,15},{8,0},{9,1},... | collective-permute-start | bytes 202760 | tf_op jit(solution)/shard_map/ppermute | solution.py:97
  99.3 6.3 %collective-permute-start.13 = (bf16[1,88,256]{2,1,0:T(8,128)(2,1)S(1)}, bf16[1,88,256]{2,1,0:T(8,128)(2,1)S(1)}, u32[]{:S(2)}, u32[]{:S(2)}) collective-permute-start(bf16[1,88,256]{2,1,0:T(8,128)(2,1)S(1)} %dynamic-slice_convert_fusion.7), channel_id=1, source_target_pairs={{0,8},{1,9},{2,10},{3,11},{4,12},{5,13},{6,14},{7,15},{8,0},{9,1},... | collective-permute-start | bytes 135176 | tf_op jit(solution)/shard_map/ppermute | solution.py:97
  106.1 10.3 %copy-start.2 = (f32[2,3,7776]{2,0,1:T(2,128)}, f32[2,3,7776]{2,0,1:T(2,128)S(1)}, u32[]{:S(2)}) copy-start(f32[2,3,7776]{2,0,1:T(2,128)S(1)} %copy.141) | copy-start | bytes 559876
where the time goes:
time: 117 us; the launch traced here: 116 us
  waiting for transfers between devices  46.9 us (40%)
  Pallas kernels  21.7 us (19%)
  starting transfers between devices  21.1 us (18%)
  blocking collectives  9.02 us (8%)
  local copies, waits for them, and re-layouts  8.95 us (8%)
  other arithmetic  7.66 us (7%)
    ppermute x10, waiting for transfers between devices, exchange(): taken = lax.ppermute(given, axis, swap_pairs(lax.axis_size(axis), distance))  27 us
    all_to_all x1, waiting for transfers between devices, share_sums(): return jnp.sum(lax.all_to_all(copies, axes, 0, 0), axis=0)  11 us
    all_to_all x1, blocking collectives, share_sums(): return jnp.sum(lax.all_to_all(copies, axes, 0, 0), axis=0)  9.02 us
    pallas_call x1, Pallas kernels, on_device(): pl.pallas_call(functools.partial(forward_kernel, plan, classes, scale), o...  8.31 us
    ppermute x2, starting transfers between devices, outward(): taken = lax.ppermute(chain[:, :amount], AXES, pairs)  8.06 us
    all_to_all x1, starting transfers between devices, share_sums(): return jnp.sum(lax.all_to_all(copies, axes, 0, 0), axis=0)  7.21 us
    pallas_call x1, Pallas kernels, on_device(): pl.pallas_call(functools.partial(pair_kernel, plan, slots_of(plan, orders...  7.15 us
    ppermute x2, waiting for transfers between devices, outward(): taken = lax.ppermute(chain[:, :amount], AXES, pairs)  6.83 us
  transfers between devices with their start and end apart: 15, of which 11 were waited for; matrix products, arithmetic and copies ran while one was open for 8% of the time, Pallas kernels for 0%

commit v1 on v0

--- a/solution.py
+++ b/solution.py
@@ -106,13 +106,15 @@
 
 
 def reduce_shares(chains, orders):
-    chains = list(chains)
-    for step in range(len(orders[0])):
+    chains, after = (list(chains), None)
+    for step in range(max(len(order) for order in orders)):
         for n, order in enumerate(orders):
-            after = chains[n - 1][1] if len(chains) > 1 else None
+            if step >= len(order):
+                continue
             kept = exchange(*chains[n], *order[step], after)
             last = step + 1 == len(order)
             chains[n] = (kept, None) if last else halve(kept, *order[step + 1])
+            after = chains[n][1] if not last else after
     return [kept for kept, _ in chains]
 
 
@@ -148,6 +150,33 @@
         self.per_group = chans // self.groups
         self.pitch = 28 if self.aligned else 32
         self.rows = round_up(self.per_group * self.pitch, 8)
+        self.half_rows = self.per_group * self.pitch // 2
+
+    def pieces(self, tasks):
+        lanes = 2 * tasks * self.chans
+        chunks = list(range(-(-lanes // 128)))
+        if tasks == 1:
+            return [(chunks, len(chunks) > 1 and 0 < lanes % 128 <= 64 and self.aligned)]
+        split = -(-2 * len(chunks) // 3)
+        return [(part, False) for part in (chunks[:split], chunks[split:]) if part]
+
+    def piece_shape(self, piece):
+        chunks, folded = piece
+        shares = self.groups // 2
+        if folded:
+            rows = (len(chunks) - 1) * self.rows + round_up(self.half_rows, 8)
+            return (shares, rows, 128)
+        return (shares, self.rows, 128 * len(chunks))
+
+    def unpack(self, piece, share):
+        chunks, folded = piece
+        share, length = (share[0], self.per_group * self.pitch)
+        if not folded:
+            return share[:length]
+        parts = [share[n * self.rows : n * self.rows + length] for n in range(len(chunks) - 1)]
+        last = share[(len(chunks) - 1) * self.rows :][: self.half_rows]
+        parts.append(jnp.concatenate([last[:, :64], last[:, 64:]], axis=0))
+        return jnp.concatenate(parts, axis=1)
 
     def planes(self, name):
         low, high = self.x[name]
@@ -605,21 +634,39 @@
                         c * chans : (c + 1) * chans, :
                     ]
     if plan.aligned:
-        kept_ref, given_ref = outs
         half = lax.rem(lax.axis_index("inline"), 2)
         tiles = plan.groups // plan.inline_count
         length = plan.per_group * plan.pitch
-        for high in range(plan.inline_count // 2):
-            for chunk, ref in enumerate(rows_refs):
-                span = slice(chunk * lanes, (chunk + 1) * lanes)
-                for target_ref, bit in ((kept_ref, half), (given_ref, 1 - half)):
-                    start = pl.multiple_of((2 * high + bit) * tiles * length, 8)
-                    block = ref.at[pl.ds(start, tiles * length + 8), :]
+        lane = lax.broadcasted_iota(jnp.int32, (round_up(plan.half_rows, 8), lanes), 1)
+
+        def share_of(ref, bit, high, j, start, count):
+            base = pl.multiple_of((2 * high + bit) * tiles * length, 8)
+            block = ref.at[pl.ds(base, tiles * length + 8), :]
+            return block[j * length + start : j * length + start + count, :]
+
+        for number, (chunks, folded) in enumerate(plan.pieces(tasks)):
+            for target_ref, bit in ((outs[2 * number], half), (outs[2 * number + 1], 1 - half)):
+                kind = target_ref.dtype
+                for high in range(plan.inline_count // 2):
                     for j in range(tiles):
-                        value = block[j * length : j * length + plan.rows, :]
-                        target_ref[slots[high * tiles + j], :, span] = value.astype(
-                            target_ref.dtype
-                        )
+                        slot = slots[number][high * tiles + j]
+                        for place, chunk in enumerate(chunks):
+                            ref = rows_refs[chunk]
+                            if folded and place == len(chunks) - 1:
+                                count = lane.shape[0]
+                                left = share_of(ref, bit, high, j, 0, count)
+                                right = share_of(ref, bit, high, j, plan.half_rows, count)
+                                value = jnp.where(lane < 64, left, pltpu.roll(right, 64, 1))
+                                span = slice(place * plan.rows, place * plan.rows + count)
+                                target_ref[slot, span, :] = value.astype(kind)
+                                continue
+                            value = share_of(ref, bit, high, j, 0, plan.rows).astype(kind)
+                            if folded:
+                                span = slice(place * plan.rows, (place + 1) * plan.rows)
+                                target_ref[slot, span, :] = value
+                            else:
+                                span = slice(place * lanes, (place + 1) * lanes)
+                                target_ref[slot, :, span] = value
     else:
         (out_ref,) = outs
 
@@ -635,7 +682,7 @@
 def pair_kernel(
     plan, slots, delta_ref, cot_ref, slope1_ref, near1_ref, near2_ref, w2t_ref, *rest
 ):
-    outs, scratch = split_refs(plan, rest)
+    outs, scratch = split_refs(plan, 2, rest)
     cot_of = lambda task, x, z: cot_ref[task, plan.index("middle", x, z)]
     backward_body(
         plan,
@@ -668,7 +715,7 @@
     w2t_ref,
     *rest,
 ):
-    outs, scratch = split_refs(plan, rest)
+    outs, scratch = split_refs(plan, 1, rest)
     delta_ref, cot_ref, spread_ref = scratch[:3]
     salt_cotangents(
         plan,
@@ -699,8 +746,8 @@
     )
 
 
-def split_refs(plan, refs):
-    count = 2 if plan.aligned else 1
+def split_refs(plan, tasks, refs):
+    count = 2 * len(plan.pieces(tasks)) if plan.aligned else 1
     return (refs[:count], refs[count:])
 
 
@@ -712,8 +759,10 @@
     chans = plan.chans
     width = round_up(2 * tasks * chans, 128)
     if plan.aligned:
-        shape = (plan.groups // 2, plan.rows, width)
-        outs = [jax.ShapeDtypeStruct(shape, jnp.float32), jax.ShapeDtypeStruct(shape, jnp.bfloat16)]
+        outs = []
+        for piece in plan.pieces(tasks):
+            for kind in (jnp.float32, jnp.bfloat16):
+                outs.append(jax.ShapeDtypeStruct(plan.piece_shape(piece), kind))
     else:
         outs = [jax.ShapeDtypeStruct((plan.groups, plan.pitch, width), jnp.float32)]
     scratch = [
@@ -826,18 +875,21 @@
 
     sums = share_sums(sums, AXES if plan.whole else ("tile",))
 
-    orders = [halving_order(0), halving_order(len(bits(tile_count)) // 2)]
+    order_of = {0: halving_order(0), 1: halving_order(1), 2: halving_order(2)}
+    pair_slots = [slots_of(plan, order_of[n]) for n in range(len(plan.pieces(2)))]
     outs, scratch = backward_shapes(plan, 2)
     pair = pl.pallas_call(
-        functools.partial(pair_kernel, plan, slots_of(plan, orders[0])),
+        functools.partial(pair_kernel, plan, pair_slots),
         out_shape=outs,
         in_specs=vmem(6),
         out_specs=vmem(len(outs)),
         scratch_shapes=scratch,
         name="pair",
     )(delta, cot, slope1, near1, near2, w2t)
+    pair = list(pair)
     if plan.aligned:
-        pair = first_halving(*pair, orders[0])
+        for n in range(len(pair) // 2):
+            pair[2 * n : 2 * n + 2] = first_halving(pair[2 * n], pair[2 * n + 1], order_of[n])
     sums, *pair = lax.optimization_barrier((sums, *pair))
     outs, scratch = backward_shapes(plan, 1)
     scratch = [
@@ -845,23 +897,32 @@
         pltpu.VMEM((1, second, chans, 128), f32),
         pltpu.VMEM((1 + classes[2], chans, 128), f32),
     ] + scratch
+    operands = (stats, sums, cols, slope2, slope1, near1, near2, w2t)
+    held = sum(
+        math.prod(ref.shape) * jnp.dtype(ref.dtype).itemsize
+        for ref in [*operands, *outs, *scratch]
+    )
+    salt_limit = max(24 << 20, 2 * held)
     salt = pl.pallas_call(
         functools.partial(
-            salt_kernel, plan, slots_of(plan, orders[1]), classes, plan.depth_total * scale
+            salt_kernel, plan, [slots_of(plan, order_of[2])], classes, plan.depth_total * scale
         ),
         out_shape=outs,
         in_specs=vmem(8),
         out_specs=vmem(len(outs)),
         scratch_shapes=scratch,
+        compiler_params=pltpu.CompilerParams(vmem_limit_bytes=salt_limit),
         name="salt",
-    )(stats, sums, cols, slope2, slope1, near1, near2, w2t)
+    )(*operands)
 
     terms = []
     if plan.aligned:
-        salt = first_halving(*salt, orders[1])
-        shared = reduce_shares([pair, salt], [order[1:] for order in orders])
-        for share, tasks in zip(shared, (2, 1)):
-            share = share[0, : plan.per_group * plan.pitch]
+        chains = [pair[-2:], salt] + ([pair[:2]] if len(pair) > 2 else [])
+        orders = [order_of[len(pair) // 2 - 1][1:], order_of[2], order_of[0][1:]][: len(chains)]
+        shares_of = reduce_shares(chains, orders)
+        pair = [plan.unpack(*each) for each in zip(plan.pieces(2), shares_of[2:] + shares_of[:1])]
+        salt = plan.unpack(plan.pieces(1)[0], shares_of[1])
+        for share, tasks in ((joined(pair, 1), 2), (salt, 1)):
             share = share.reshape(plan.per_group, plan.pitch, -1)
             share = share[:, :27, : 2 * tasks * chans].reshape(-1, 2, tasks, chans)
             terms.append(share.transpose(1, 2, 0, 3).reshape(2, tasks, -1))
@@ -873,10 +934,10 @@
         flat = jnp.concatenate(terms, axis=1).transpose(2, 0, 1, 3)
         left = [(axis, d) for axis in AXES for d in reversed(bits(lax.axis_size(axis)))]
         flat = flat.reshape((2,) * len(left) + flat.shape[1:])
-        places = [left.index(entry) for entry in orders[0]]
+        places = [left.index(entry) for entry in order_of[0]]
         flat = flat.transpose(places + [len(left), len(left) + 1, len(left) + 2])
         flat = flat.reshape((-1,) + flat.shape[len(left) :])
-        grads = reduce_shares([halve(flat, *orders[0][0])], orders[:1])[0][0]
+        grads = reduce_shares([halve(flat, *order_of[0][0])], [order_of[0]])[0][0]
     gram = jnp.sum(grads[:, :, None, :] * grads[:, None, :, :], axis=3)
     gram = share_sums(gram.reshape(2, 9), AXES).reshape(2, 3, 3) / (27 * chans * chans)
     return (grads, gram)

time: 117 us -> 112 us (0.957)
  waiting for transfers between devices: 46.9 us -> 38.3 us
  starting transfers between devices: 21.1 us -> 26.1 us
  Pallas kernels: 21.7 us -> 18.6 us
  local copies, waits for them, and re-layouts: 8.95 us -> 11.4 us
  other arithmetic: 7.66 us -> 6.38 us
    ppermute x10 -> x15, waiting for transfers between devices: 27 us -> 20.4 us  [exchange(): taken = lax.ppermute(given, axis, swap_pairs(lax.axis_size(axis), distance))]
    ppermute x10 -> x15, starting transfers between devices: 5.19 us -> 10.1 us  [exchange(): taken = lax.ppermute(given, axis, swap_pairs(lax.axis_size(axis), distance))]
    pallas_call x2, Pallas kernels: 13.4 us -> 10.4 us  [the longest x1 7.2 us: on_device(): pl.pallas_call(functools.partial(pair_kernel, plan, pair_slots), out_shap...]
    all_to_all x1, waiting for transfers between devices: 11 us -> 8.93 us  [share_sums(): return jnp.sum(lax.all_to_all(copies, axes, 0, 0), axis=0)]
    convert_element_type x8 -> x12, local copies, waits for them, and re-layouts: 0.26 us -> 1.71 us  [halve(): lax.dynamic_slice_in_dim(kept, (1 - bit) * half, half, 0)]
    unnamed x19 -> x35, local copies, waits for them, and re-layouts: 2.43 us -> 3.31 us
    add x10 -> x15, other arithmetic: 3.62 us -> 2.91 us  [exchange(): return kept + taken.astype(jnp.float32)]
  transfers between devices with their start and end apart: 15 -> 20, of which waited for: 11 -> 14; matrix products, arithmetic and copies ran while one was open for 8% -> 10% of each run, Pallas kernels for 0% -> 0%
where the time goes in v1:
time: 112 us; the launch traced here: 111 us
  waiting for transfers between devices  38.3 us (34%)
  starting transfers between devices  26.1 us (23%)
  Pallas kernels  18.6 us (17%)
  local copies, waits for them, and re-layouts  11.4 us (10%)
  blocking collectives  9.45 us (8%)
  other arithmetic  6.38 us (6%)
  between operations  1.19 us (1%)
    ppermute x15, waiting for transfers between devices, exchange(): taken = lax.ppermute(given, axis, swap_pairs(lax.axis_size(axis), distance))  20.4 us
    ppermute x15, starting transfers between devices, exchange(): taken = lax.ppermute(given, axis, swap_pairs(lax.axis_size(axis), distance))  10.1 us
    all_to_all x1, blocking collectives, share_sums(): return jnp.sum(lax.all_to_all(copies, axes, 0, 0), axis=0)  9.45 us
    all_to_all x1, waiting for transfers between devices, share_sums(): return jnp.sum(lax.all_to_all(copies, axes, 0, 0), axis=0)  8.93 us
    pallas_call x1, Pallas kernels, on_device(): pl.pallas_call(functools.partial(forward_kernel, plan, classes, scale), o...  8.25 us
    ppermute x2, starting transfers between devices, outward(): taken = lax.ppermute(chain[:, :amount], AXES, pairs)  8.06 us
    all_to_all x1, starting transfers between devices, share_sums(): return jnp.sum(lax.all_to_all(copies, axes, 0, 0), axis=0)  7.24 us
    pallas_call x1, Pallas kernels, on_device(): pl.pallas_call(functools.partial(pair_kernel, plan, pair_slots), out_shap...  7.2 us
  transfers between devices with their start and end apart: 20, of which 14 were waited for; matrix products, arithmetic and copies ran while one was open for 10% of the time, Pallas kernels for 0%

profile of v1, /device:TPU:0, one launch (start us, length us, event | category | flops | bytes accessed | tf_op | source)
XLA Modules:
  0.0 111.4 jit_solution(4835328451249343673)
XLA Ops:
  2.1 0.9 copy.149
  3.6 1.0 collective-permute-done
  4.7 4.7 %collective-permute-start.1 = (bf16[4,2,104,128]{3,2,1,0:T(8,128)(2,1)S(1)}, bf16[4,2,104,128]{3,2,1,0:T(8,128)(2,1)S(1)}, u32[]{:S(2)}, u32[]{:S(2)}) collective-permute-start(bf16[4,2,104,128]{3,2,1,0:T(8,128)(2,1)S(1)} %reverse_select_fusion), channel_id=1, source_target_pairs={{0,1},{1,2},{2,3},{3,4},{4,5},{5,6},{6,7},{7,8},{8,9},{9,10},{10,1... | collective-permute-start | bytes 638984 | tf_op jit(solution)/shard_map/ppermute | solution.py:63
  10.3 1.1 copy.128.refs_3_
  12.0 3.1 %collective-permute-done.1 = bf16[4,2,104,128]{3,2,1,0:T(8,128)(2,1)S(1)} collective-permute-done((bf16[4,2,104,128]{3,2,1,0:T(8,128)(2,1)S(1)}, bf16[4,2,104,128]{3,2,1,0:T(8,128)(2,1)S(1)}, u32[]{:S(2)}, u32[]{:S(2)}) %collective-permute-start.1) | collective-permute-done | bytes 213024 | tf_op jit(solution)/shard_map/ppermute | solution.py:63
  15.1 3.3 %collective-permute-start.2 = (bf16[4,3,104,128]{3,2,1,0:T(8,128)(2,1)S(1)}, bf16[4,3,104,128]{3,2,1,0:T(8,128)(2,1)S(1)}, u32[]{:S(2)}, u32[]{:S(2)}) collective-permute-start(bf16[4,3,104,128]{3,2,1,0:T(8,128)(2,1)S(1)} %pad_maximum_fusion), channel_id=1, source_target_pairs={{0,2},{1,3},{2,4},{3,5},{4,6},{5,7},{6,8},{7,9},{8,10},{9,11},{10,... | collective-permute-start | bytes 958472 | tf_op jit(solution)/shard_map/ppermute | solution.py:63
  18.7 1.1 copy.131.w2t_ref
  19.8 1.1 copy.129.refs_4_
  20.9 3.8 %collective-permute-done.2 = bf16[4,3,104,128]{3,2,1,0:T(8,128)(2,1)S(1)} collective-permute-done((bf16[4,3,104,128]{3,2,1,0:T(8,128)(2,1)S(1)}, bf16[4,3,104,128]{3,2,1,0:T(8,128)(2,1)S(1)}, u32[]{:S(2)}, u32[]{:S(2)}) %collective-permute-start.2) | collective-permute-done | bytes 319520 | tf_op jit(solution)/shard_map/ppermute | solution.py:63
  25.6 1.2 %collective-permute-done.3 = bf16[4,5,104,128]{3,2,1,0:T(8,128)(2,1)S(1)} collective-permute-done((bf16[4,5,104,128]{3,2,1,0:T(8,128)(2,1)S(1)}, bf16[4,5,104,128]{3,2,1,0:T(8,128)(2,1)S(1)}, u32[]{:S(2)}, u32[]{:S(2)}) %collective-permute-start.3) | collective-permute-done | bytes 532512 | tf_op jit(solution)/shard_map/ppermute | solution.py:73
  26.8 0.8 copy-done.13
  27.6 8.2 %forward.1 = (bf16[12,288,128]{2,1,0:T(8,128)(2,1)}, bf16[12,288,128]{2,1,0:T(8,128)(2,1)}, f32[4,96,128]{2,1,0:T(8,128)}, f32[12,96,128]{2,1,0:T(8,128)}, bf16[...) custom-call(bf16[8,104,128]{2,1,0:T(8,128)(2,1)} %bitcast.39, ...), custom_call_target="tpu_custom_call" | custom-call | tf_op jit(solution)/shard_map/forward/pallas_call | solution.py:853
  35.8 7.2 %pair.1 = (f32[16,88,256]{2,1,0:T(8,128)}, bf16[16,88,256]{2,1,0:T(8,128)(2,1)}, f32[16,88,128]{2,1,0:T(8,128)}, bf16[16,88,128]{2,1,0:T(8,128)(2,1)}) custom-call(bf16[2,12,96,128]{3,2,1,0:T(8,128)(2,1)} %get-tuple-element.47.delta_ref, f32[2,4,96,128]{3,2,1,0:T(8,128)} %get-tuple-element.48.cot_ref, f32[4,96,128]{2,1,0:T(8,128)} %get-tuple-element.49.slope1_ref, ...), custom_call_target="tpu_custom_call" | custom-call | tf_op jit(solution)/shard_map/pair/pallas_call | solution.py:881
  44.2 7.2 %all-to-all-start = ((f32[32,16,128]{2,1,0:T(8,128)}), f32[32,16,128]{2,1,0:T(8,128)S(1)}, u32[]{:S(2)}, u32[]{:S(2)}) async-start(f32[32,16,128]{2,1,0:T(8,128)} %broadcast_in_dim.13), calls=%async_computation | async-start | bytes 524288 | tf_op jit(solution)/shard_map/all_to_all | solution.py:79
  51.5 1.3 %convert_add_fusion.3 = f32[16,88,128]{2,1,0:T(8,128)S(1)} fusion(f32[16,88,128]{2,1,0:T(8,128)} %get-tuple-element.55, bf16[16,88,128]{2,1,0:T(8,128)(2,1)S(1)} %collective-permute-done.5), kind=kLoop, calls=%fused_computation.3 | loop fusion | flops 360448 | bytes 1802240 | tf_op jit(solution)/shard_map/add | solution.py:100
  53.6 8.9 %all-to-all-done = f32[32,16,128]{2,1,0:T(8,128)S(1)} async-done(((f32[32,16,128]{2,1,0:T(8,128)}), f32[32,16,128]{2,1,0:T(8,128)S(1)}, u32[]{:S(2)}, u32[]{:S(2)}) %all-to-all-start) | async-done | bytes 262176 | tf_op jit(solution)/shard_map/all_to_all | solution.py:79
  64.5 3.2 %salt.1 = (f32[16,136,128]{2,1,0:T(8,128)S(1)}, bf16[16,136,128]{2,1,0:T(8,128)(2,1)S(1)}) custom-call(f32[12,8,128]{2,1,0:T(8,128)S(1)} %copy-done.6, f32[16,128]{1,0:T(8,128)S(1)} %reduce_sum.27.sums_ref, f32[96,16]{1,0:T(8,128)S(1)} %copy-done.5, f32[12,96,128]{2,1,0:T(8,128)S(1)} %copy-done.4, f32[4,96,128]{2,1,0:T(8,128)S(1)} %copy-done.3, ...), custom_call_target="tpu_custom_call" | custom-call | tf_op jit(solution)/shard_map/salt/pallas_call | solution.py:906
  68.1 0.8 collective-permute-start.6
  68.9 6.2 %collective-permute-done.8 = bf16[8,88,128]{2,1,0:T(8,128)(2,1)} collective-permute-done((bf16[8,88,128]{2,1,0:T(8,128)(2,1)}, bf16[8,88,128]{2,1,0:T(8,128)(2,1)}, u32[]{:S(2)}, u32[]{:S(2)}) %collective-permute-start.8) | collective-permute-done | bytes 180256 | tf_op jit(solution)/shard_map/ppermute | solution.py:97
  75.1 1.0 convert_add_fusion.6
  77.3 2.0 %collective-permute-done.6 = bf16[8,88,256]{2,1,0:T(8,128)(2,1)S(1)} collective-permute-done((bf16[8,88,256]{2,1,0:T(8,128)(2,1)}, bf16[8,88,256]{2,1,0:T(8,128)(2,1)S(1)}, u32[]{:S(2)}, u32[]{:S(2)}) %collective-permute-start.6) | collective-permute-done | bytes 360480 | tf_op jit(solution)/shard_map/ppermute | solution.py:97
  79.5 2.1 %collective-permute-start.9 = (bf16[4,88,256]{2,1,0:T(8,128)(2,1)S(1)}, bf16[4,88,256]{2,1,0:T(8,128)(2,1)S(1)}, u32[]{:S(2)}, u32[]{:S(2)}) collective-permute-start(bf16[4,88,256]{2,1,0:T(8,128)(2,1)S(1)} %dynamic-slice_convert_fusion.2), channel_id=1, source_target_pairs={{0,2},{1,3},{2,0},{3,1},{4,6},{5,7},{6,4},{7,5},{8,10},{9,11},{10,... | collective-permute-start | bytes 540680 | tf_op jit(solution)/shard_map/ppermute | solution.py:97
  81.8 3.3 %collective-permute-done.10 = bf16[8,136,128]{2,1,0:T(8,128)(2,1)S(1)} collective-permute-done((bf16[8,136,128]{2,1,0:T(8,128)(2,1)S(1)}, bf16[8,136,128]{2,1,0:T(8,128)(2,1)S(1)}, u32[]{:S(2)}, u32[]{:S(2)}) %collective-permute-start.10) | collective-permute-done | bytes 278560 | tf_op jit(solution)/shard_map/ppermute | solution.py:97
  85.1 1.8 %collective-permute-start.13 = (bf16[4,136,128]{2,1,0:T(8,128)(2,1)S(1)}, bf16[4,136,128]{2,1,0:T(8,128)(2,1)S(1)}, u32[]{:S(2)}, u32[]{:S(2)}) collective-permute-start(bf16[4,136,128]{2,1,0:T(8,128)(2,1)S(1)} %dynamic-slice_convert_fusion.4), channel_id=1, source_target_pairs={{0,1},{1,0},{2,3},{3,2},{4,5},{5,4},{6,7},{7,6},{8,9},{9,8},{10,11... | collective-permute-start | bytes 417800 | tf_op jit(solution)/shard_map/ppermute | solution.py:97
  87.4 1.4 %collective-permute-start.17 = (bf16[1,88,128]{2,1,0:T(8,128)(2,1)S(1)}, bf16[1,88,128]{2,1,0:T(8,128)(2,1)S(1)}, u32[]{:S(2)}, u32[]{:S(2)}) collective-permute-start(bf16[1,88,128]{2,1,0:T(8,128)(2,1)S(1)} %dynamic-slice_convert_fusion.11), channel_id=1, source_target_pairs={{0,8},{1,9},{2,10},{3,11},{4,12},{5,13},{6,14},{7,15},{8,0},{9,1},... | collective-permute-start | bytes 67592 | tf_op jit(solution)/shard_map/ppermute | solution.py:97
  88.7 1.5 %collective-permute-done.13 = bf16[4,136,128]{2,1,0:T(8,128)(2,1)S(1)} collective-permute-done((bf16[4,136,128]{2,1,0:T(8,128)(2,1)S(1)}, bf16[4,136,128]{2,1,0:T(8,128)(2,1)S(1)}, u32[]{:S(2)}, u32[]{:S(2)}) %collective-permute-start.13) | collective-permute-done | bytes 139296 | tf_op jit(solution)/shard_map/ppermute | solution.py:97
  91.7 0.9 collective-permute-done.17
  92.7 2.0 %collective-permute-done.16 = bf16[2,136,128]{2,1,0:T(8,128)(2,1)S(1)} collective-permute-done((bf16[2,136,128]{2,1,0:T(8,128)(2,1)S(1)}, bf16[2,136,128]{2,1,0:T(8,128)(2,1)S(1)}, u32[]{:S(2)}, u32[]{:S(2)}) %collective-permute-start.16) | collective-permute-done | bytes 69664 | tf_op jit(solution)/shard_map/ppermute | solution.py:97
  94.7 0.8 collective-permute-start.18
  95.6 1.5 %collective-permute-done.15 = bf16[1,88,256]{2,1,0:T(8,128)(2,1)S(1)} collective-permute-done((bf16[1,88,256]{2,1,0:T(8,128)(2,1)S(1)}, bf16[1,88,256]{2,1,0:T(8,128)(2,1)S(1)}, u32[]{:S(2)}, u32[]{:S(2)}) %collective-permute-start.15) | collective-permute-done | bytes 45088 | tf_op jit(solution)/shard_map/ppermute | solution.py:97
  97.6 2.4 %collective-permute-done.18 = bf16[1,136,128]{2,1,0:T(8,128)(2,1)S(1)} collective-permute-done((bf16[1,136,128]{2,1,0:T(8,128)(2,1)S(1)}, bf16[1,136,128]{2,1,0:T(8,128)(2,1)S(1)}, u32[]{:S(2)}, u32[]{:S(2)}) %collective-permute-start.18) | collective-permute-done | bytes 34848 | tf_op jit(solution)/shard_map/ppermute | solution.py:97
  101.2 9.4 %all_to_all.10 = f32[32,2,9]{2,1,0:T(2,128)S(1)} all-to-all(f32[32,2,9]{2,1,0:T(2,128)S(1)} %broadcast_in_dim.14), channel_id=1, replica_groups=mesh['inline'=2,'tile'=16] {'inline','tile'}, dimensions={0} | all-to-all | bytes 4608 | tf_op jit(solution)/shard_map/all_to_all | solution.py:79
  (120 shorter events, 14.9 us)
Async XLA Ops:
  0.6 9.6 %copy-start.12 = (bf16[96,27,96]{2,0,1:T(8,128)(2,1)S(1)}, bf16[96,27,96]{2,0,1:T(8,128)(2,1)}, u32[]{:S(2)}) copy-start(bf16[96,27,96]{2,0,1:T(8,128)(2,1)} %param.11) | copy-start | bytes 1492996
  3.1 1.5 %collective-permute-start = (bf16[2,2,104,128]{3,2,1,0:T(8,128)(2,1)S(1)}, bf16[2,2,104,128]{3,2,1,0:T(8,128)(2,1)S(1)}, u32[]{:S(2)}, u32[]{:S(2)}) collective-permute-start(bf16[2,2,104,128]{3,2,1,0:T(8,128)(2,1)S(1)} %pad_maximum_fusion.4), channel_id=1, source_target_pairs={{0,16},{16,0},{1,17},{17,1},{2,18},{18,2},{3,19},{19,3},{4,20},{20... | collective-permute-start | bytes 319496 | tf_op jit(solution)/shard_map/ppermute | solution.py:838
  3.6 14.8 %copy-start.7 = (bf16[96,27,96]{2,0,1:T(8,128)(2,1)S(1)}, bf16[96,27,96]{2,0,1:T(8,128)(2,1)}, u32[]{:S(2)}) copy-start(bf16[96,27,96]{2,0,1:T(8,128)(2,1)} %param.12) | copy-start | bytes 1492996
  4.6 14.1 %copy-start.8 = (bf16[4,2,104,128]{3,2,1,0:T(8,128)(2,1)}, bf16[4,2,104,128]{3,2,1,0:T(8,128)(2,1)S(1)}, u32[]{:S(2)}) copy-start(bf16[4,2,104,128]{3,2,1,0:T(8,128)(2,1)S(1)} %pad_maximum_fusion.2) | copy-start | bytes 638980
  4.7 10.4 %collective-permute-start.1 = (bf16[4,2,104,128]{3,2,1,0:T(8,128)(2,1)S(1)}, bf16[4,2,104,128]{3,2,1,0:T(8,128)(2,1)S(1)}, u32[]{:S(2)}, u32[]{:S(2)}) collective-permute-start(bf16[4,2,104,128]{3,2,1,0:T(8,128)(2,1)S(1)} %reverse_select_fusion), channel_id=1, source_target_pairs={{0,1},{1,2},{2,3},{3,4},{4,5},{5,6},{6,7},{7,8},{8,9},{9,10},{10,1... | collective-permute-start | bytes 638984 | tf_op jit(solution)/shard_map/ppermute | solution.py:63
  15.1 9.6 %collective-permute-start.2 = (bf16[4,3,104,128]{3,2,1,0:T(8,128)(2,1)S(1)}, bf16[4,3,104,128]{3,2,1,0:T(8,128)(2,1)S(1)}, u32[]{:S(2)}, u32[]{:S(2)}) collective-permute-start(bf16[4,3,104,128]{3,2,1,0:T(8,128)(2,1)S(1)} %pad_maximum_fusion), channel_id=1, source_target_pairs={{0,2},{1,3},{2,4},{3,5},{4,6},{5,7},{6,8},{7,9},{8,10},{9,11},{10,... | collective-permute-start | bytes 958472 | tf_op jit(solution)/shard_map/ppermute | solution.py:63
  24.8 2.0 %copy-start.11 = (bf16[4,5,104,128]{3,2,1,0:T(8,128)(2,1)}, bf16[4,5,104,128]{3,2,1,0:T(8,128)(2,1)S(1)}, u32[]{:S(2)}) copy-start(bf16[4,5,104,128]{3,2,1,0:T(8,128)(2,1)S(1)} %constant_dynamic-update-slice_fusion) | copy-start | bytes 1597444
  24.8 2.0 %collective-permute-start.3 = (bf16[4,5,104,128]{3,2,1,0:T(8,128)(2,1)S(1)}, bf16[4,5,104,128]{3,2,1,0:T(8,128)(2,1)S(1)}, u32[]{:S(2)}, u32[]{:S(2)}) collective-permute-start(bf16[4,5,104,128]{3,2,1,0:T(8,128)(2,1)S(1)} %constant_dynamic-update-slice_fusion), channel_id=1, source_target_pairs={{0,16},{16,0},{1,17},{17,1},{2,18},{18,2},{3,19},{19,3},{4,20},{20... | collective-permute-start | bytes 1597448 | tf_op jit(solution)/shard_map/ppermute | solution.py:73
  35.8 7.7 %copy-start.14 = (f32[16,128]{1,0:T(8,128)S(1)}, f32[16,128]{1,0:T(8,128)}, u32[]{:S(2)}) copy-start(f32[16,128]{1,0:T(8,128)} %get-tuple-element.46) | copy-start | bytes 24580
  43.0 8.5 %collective-permute-start.5 = (bf16[16,88,128]{2,1,0:T(8,128)(2,1)}, bf16[16,88,128]{2,1,0:T(8,128)(2,1)S(1)}, u32[]{:S(2)}, u32[]{:S(2)}) collective-permute-start(bf16[16,88,128]{2,1,0:T(8,128)(2,1)} %get-tuple-element.56), channel_id=1, source_target_pairs={{0,16},{16,0},{1,17},{17,1},{2,18},{18,2},{3,19},{19,3},{4,20},{20... | collective-permute-start | bytes 1081352 | tf_op jit(solution)/shard_map/ppermute | solution.py:97
  43.2 19.4 %collective-permute-start.4 = (bf16[16,88,256]{2,1,0:T(8,128)(2,1)}, bf16[16,88,256]{2,1,0:T(8,128)(2,1)S(1)}, u32[]{:S(2)}, u32[]{:S(2)}) collective-permute-start(bf16[16,88,256]{2,1,0:T(8,128)(2,1)} %get-tuple-element.54), channel_id=1, source_target_pairs={{0,16},{16,0},{1,17},{17,1},{2,18},{18,2},{3,19},{19,3},{4,20},{20... | collective-permute-start | bytes 2162696 | tf_op jit(solution)/shard_map/ppermute | solution.py:97
  44.2 18.3 %all-to-all-start = ((f32[32,16,128]{2,1,0:T(8,128)}), f32[32,16,128]{2,1,0:T(8,128)S(1)}, u32[]{:S(2)}, u32[]{:S(2)}) async-start(f32[32,16,128]{2,1,0:T(8,128)} %broadcast_in_dim.13), calls=%async_computation | async-start | bytes 524288 | tf_op jit(solution)/shard_map/all_to_all | solution.py:79
  51.5 11.0 %copy-start.10 = (f32[16,88,256]{2,1,0:T(8,128)S(1)}, f32[16,88,256]{2,1,0:T(8,128)}, u32[]{:S(2)}) copy-start(f32[16,88,256]{2,1,0:T(8,128)} %get-tuple-element.53) | copy-start | bytes 4325380
  62.8 1.4 %copy-start = (bf16[3,96,864]{2,1,0:T(8,128)(2,1)S(1)}, bf16[3,96,864]{2,1,0:T(8,128)(2,1)}, u32[]{:S(2)}) copy-start(bf16[3,96,864]{2,1,0:T(8,128)(2,1)} %copy.131.w2t_ref) | copy-start | bytes 1492996
  62.8 1.7 %copy-start.1 = (bf16[12,288,128]{2,1,0:T(8,128)(2,1)S(1)}, bf16[12,288,128]{2,1,0:T(8,128)(2,1)}, u32[]{:S(2)}) copy-start(bf16[12,288,128]{2,1,0:T(8,128)(2,1)} %get-tuple-element.50.near1_ref) | copy-start | bytes 2654212
  62.8 1.7 %copy-start.3 = (f32[4,96,128]{2,1,0:T(8,128)S(1)}, f32[4,96,128]{2,1,0:T(8,128)}, u32[]{:S(2)}) copy-start(f32[4,96,128]{2,1,0:T(8,128)} %get-tuple-element.49.slope1_ref) | copy-start | bytes 589828
  62.8 1.7 %copy-start.5 = (f32[96,16]{1,0:T(8,128)S(1)}, f32[96,16]{1,0:T(8,128)}, u32[]{:S(2)}) copy-start(f32[96,16]{1,0:T(8,128)} %get-tuple-element.45.refs_6_.cols_ref) | copy-start | bytes 18436
  62.8 1.7 %copy-start.6 = (f32[12,8,128]{2,1,0:T(8,128)S(1)}, f32[12,8,128]{2,1,0:T(8,128)}, u32[]{:S(2)}) copy-start(f32[12,8,128]{2,1,0:T(8,128)} %get-tuple-element.59.stats_ref) | copy-start | bytes 147460
  67.7 8.7 %collective-permute-start.7 = (bf16[16,136,128]{2,1,0:T(8,128)(2,1)S(1)}, bf16[16,136,128]{2,1,0:T(8,128)(2,1)S(1)}, u32[]{:S(2)}, u32[]{:S(2)}) collective-permute-start(bf16[16,136,128]{2,1,0:T(8,128)(2,1)S(1)} %get-tuple-element.63), channel_id=1, source_target_pairs={{0,16},{16,0},{1,17},{17,1},{2,18},{18,2},{3,19},{19,3},{4,20},{20... | collective-permute-start | bytes 1671176 | tf_op jit(solution)/shard_map/ppermute | solution.py:97
  67.8 7.3 %collective-permute-start.8 = (bf16[8,88,128]{2,1,0:T(8,128)(2,1)}, bf16[8,88,128]{2,1,0:T(8,128)(2,1)}, u32[]{:S(2)}, u32[]{:S(2)}) collective-permute-start(bf16[8,88,128]{2,1,0:T(8,128)(2,1)} %dynamic-slice_convert_fusion.3), channel_id=1, source_target_pairs={{0,2},{1,3},{2,0},{3,1},{4,6},{5,7},{6,4},{7,5},{8,10},{9,11},{10,... | collective-permute-start | bytes 540680 | tf_op jit(solution)/shard_map/ppermute | solution.py:97
  68.1 11.3 %collective-permute-start.6 = (bf16[8,88,256]{2,1,0:T(8,128)(2,1)}, bf16[8,88,256]{2,1,0:T(8,128)(2,1)S(1)}, u32[]{:S(2)}, u32[]{:S(2)}) collective-permute-start(bf16[8,88,256]{2,1,0:T(8,128)(2,1)} %dynamic-slice_convert_fusion), channel_id=1, source_target_pairs={{0,1},{1,0},{2,3},{3,2},{4,5},{5,4},{6,7},{7,6},{8,9},{9,8},{10,11... | collective-permute-start | bytes 1081352 | tf_op jit(solution)/shard_map/ppermute | solution.py:97
  76.1 5.5 %collective-permute-start.11 = (bf16[4,88,128]{2,1,0:T(8,128)(2,1)S(1)}, bf16[4,88,128]{2,1,0:T(8,128)(2,1)S(1)}, u32[]{:S(2)}, u32[]{:S(2)}) collective-permute-start(bf16[4,88,128]{2,1,0:T(8,128)(2,1)S(1)} %dynamic-slice_convert_fusion.6), channel_id=1, source_target_pairs={{0,1},{1,0},{2,3},{3,2},{4,5},{5,4},{6,7},{7,6},{8,9},{9,8},{10,11... | collective-permute-start | bytes 270344 | tf_op jit(solution)/shard_map/ppermute | solution.py:97
  76.6 8.4 %collective-permute-start.10 = (bf16[8,136,128]{2,1,0:T(8,128)(2,1)S(1)}, bf16[8,136,128]{2,1,0:T(8,128)(2,1)S(1)}, u32[]{:S(2)}, u32[]{:S(2)}) collective-permute-start(bf16[8,136,128]{2,1,0:T(8,128)(2,1)S(1)} %dynamic-slice_convert_fusion.1), channel_id=1, source_target_pairs={{0,4},{1,5},{2,6},{3,7},{4,0},{5,1},{6,2},{7,3},{8,12},{9,13},{10,... | collective-permute-start | bytes 835592 | tf_op jit(solution)/shard_map/ppermute | solution.py:97
  79.5 7.4 %collective-permute-start.9 = (bf16[4,88,256]{2,1,0:T(8,128)(2,1)S(1)}, bf16[4,88,256]{2,1,0:T(8,128)(2,1)S(1)}, u32[]{:S(2)}, u32[]{:S(2)}) collective-permute-start(bf16[4,88,256]{2,1,0:T(8,128)(2,1)S(1)} %dynamic-slice_convert_fusion.2), channel_id=1, source_target_pairs={{0,2},{1,3},{2,0},{3,1},{4,6},{5,7},{6,4},{7,5},{8,10},{9,11},{10,... | collective-permute-start | bytes 540680 | tf_op jit(solution)/shard_map/ppermute | solution.py:97
  81.7 5.7 %collective-permute-start.14 = (bf16[2,88,128]{2,1,0:T(8,128)(2,1)S(1)}, bf16[2,88,128]{2,1,0:T(8,128)(2,1)S(1)}, u32[]{:S(2)}, u32[]{:S(2)}) collective-permute-start(bf16[2,88,128]{2,1,0:T(8,128)(2,1)S(1)} %dynamic-slice_convert_fusion.9), channel_id=1, source_target_pairs={{0,4},{1,5},{2,6},{3,7},{4,0},{5,1},{6,2},{7,3},{8,12},{9,13},{10,... | collective-permute-start | bytes 135176 | tf_op jit(solution)/shard_map/ppermute | solution.py:97
  85.1 5.1 %collective-permute-start.13 = (bf16[4,136,128]{2,1,0:T(8,128)(2,1)S(1)}, bf16[4,136,128]{2,1,0:T(8,128)(2,1)S(1)}, u32[]{:S(2)}, u32[]{:S(2)}) collective-permute-start(bf16[4,136,128]{2,1,0:T(8,128)(2,1)S(1)} %dynamic-slice_convert_fusion.4), channel_id=1, source_target_pairs={{0,1},{1,0},{2,3},{3,2},{4,5},{5,4},{6,7},{7,6},{8,9},{9,8},{10,11... | collective-permute-start | bytes 417800 | tf_op jit(solution)/shard_map/ppermute | solution.py:97
  87.0 4.6 %collective-permute-start.12 = (bf16[2,88,256]{2,1,0:T(8,128)(2,1)S(1)}, bf16[2,88,256]{2,1,0:T(8,128)(2,1)S(1)}, u32[]{:S(2)}, u32[]{:S(2)}) collective-permute-start(bf16[2,88,256]{2,1,0:T(8,128)(2,1)S(1)} %dynamic-slice_convert_fusion.5), channel_id=1, source_target_pairs={{0,4},{1,5},{2,6},{3,7},{4,0},{5,1},{6,2},{7,3},{8,12},{9,13},{10,... | collective-permute-start | bytes 270344 | tf_op jit(solution)/shard_map/ppermute | solution.py:97
  87.4 5.3 %collective-permute-start.17 = (bf16[1,88,128]{2,1,0:T(8,128)(2,1)S(1)}, bf16[1,88,128]{2,1,0:T(8,128)(2,1)S(1)}, u32[]{:S(2)}, u32[]{:S(2)}) collective-permute-start(bf16[1,88,128]{2,1,0:T(8,128)(2,1)S(1)} %dynamic-slice_convert_fusion.11), channel_id=1, source_target_pairs={{0,8},{1,9},{2,10},{3,11},{4,12},{5,13},{6,14},{7,15},{8,0},{9,1},... | collective-permute-start | bytes 67592 | tf_op jit(solution)/shard_map/ppermute | solution.py:97
  90.3 4.4 %collective-permute-start.16 = (bf16[2,136,128]{2,1,0:T(8,128)(2,1)S(1)}, bf16[2,136,128]{2,1,0:T(8,128)(2,1)S(1)}, u32[]{:S(2)}, u32[]{:S(2)}) collective-permute-start(bf16[2,136,128]{2,1,0:T(8,128)(2,1)S(1)} %dynamic-slice_convert_fusion.7), channel_id=1, source_target_pairs={{0,2},{1,3},{2,0},{3,1},{4,6},{5,7},{6,4},{7,5},{8,10},{9,11},{10,... | collective-permute-start | bytes 208904 | tf_op jit(solution)/shard_map/ppermute | solution.py:97
  91.6 5.5 %collective-permute-start.15 = (bf16[1,88,256]{2,1,0:T(8,128)(2,1)S(1)}, bf16[1,88,256]{2,1,0:T(8,128)(2,1)S(1)}, u32[]{:S(2)}, u32[]{:S(2)}) collective-permute-start(bf16[1,88,256]{2,1,0:T(8,128)(2,1)S(1)} %dynamic-slice_convert_fusion.8), channel_id=1, source_target_pairs={{0,8},{1,9},{2,10},{3,11},{4,12},{5,13},{6,14},{7,15},{8,0},{9,1},... | collective-permute-start | bytes 135176 | tf_op jit(solution)/shard_map/ppermute | solution.py:97
  94.7 5.3 %collective-permute-start.18 = (bf16[1,136,128]{2,1,0:T(8,128)(2,1)S(1)}, bf16[1,136,128]{2,1,0:T(8,128)(2,1)S(1)}, u32[]{:S(2)}, u32[]{:S(2)}) collective-permute-start(bf16[1,136,128]{2,1,0:T(8,128)(2,1)S(1)} %dynamic-slice_convert_fusion.10), channel_id=1, source_target_pairs={{0,8},{1,9},{2,10},{3,11},{4,12},{5,13},{6,14},{7,15},{8,0},{9,1},... | collective-permute-start | bytes 104456 | tf_op jit(solution)/shard_map/ppermute | solution.py:97
  100.7 10.7 %copy-start.9 = (f32[2,3,7776]{2,0,1:T(2,128)}, f32[2,3,7776]{2,0,1:T(2,128)S(1)}, u32[]{:S(2)}) copy-start(f32[2,3,7776]{2,0,1:T(2,128)S(1)} %copy.141) | copy-start | bytes 559876
  (3 other events, 3.4 us)
